TPU v7x, 128 devices: a whole 4x4x4 slice. The times are simulated.
128 devices in a mesh: col: 8 (over y, core), row: 16 (over z, x).
Axes of the slice: x: 4, y: 4, z: 4, core: 2. Of those that a mesh axis runs over, the one named last changes fastest.
Arguments:
- multipoles: float32 [64, 131072], P(None, ('row', 'col')), may hold values from -6 to 6
- parent_locals: float32 [64, 131072], P(None, ('row', 'col')), may hold values from -6 to 6
- operators: float32 [316, 64, 64], replicated, may hold values from -0.125 to 0.125
- pair_target: int32 [316, 16384], P(None, ('row', 'col')), may hold values from 0 to 1023
- pair_partner: int32 [316, 16384], P(None, ('row', 'col')), may hold values from 0 to 9215, as said below
- pair_count: int32 [128, 316], P(('row', 'col')), may hold values from 1 to 128, as said below
- send_cells: int32 [128, 8192], P(('row', 'col')), may hold values from 0 to 1023, as said below
- send_count: int32 [128, 128], P(('row', 'col')), may hold values from 32 to 64, as said below
Outputs:
- locals_out: float32 [64, 131072], P(None, ('row', 'col'))
Inputs may be any that keep to these rules, and one draw needn't show every extreme that they name: pair_count[d, k] live pairs stand first in the positions of offset k on device d; some device has 128 live pairs at every offset. send_count[s, d] is the number of live slots, counted from the first, of the 64 slots that device s sends to device d; every device receives 64 live slots from some device. send_cells[s, d * 64 + j] is the local cell of device s in slot j of what it sends to device d; the slots sent to one device name distinct cells. `pair_partner`: A value p below 1024 names a local cell other than the pair's target; a value p at or above names slot (p - 1024) % 64 sent by device (p - 1024) // 64 to the pair's device, and that slot is live.
All inputs are finite; a program needn't handle non-finite values.
Results may differ from a plain program's by a relative error of at most 0.0003.
Values sent between devices are 32-bit elements; how exact they have to be, the bound alone decides.
No kernel may reach another device: no remote copies, remote signals or barrier semaphores. Data moves between devices by JAX's collectives and lax.ppermute only.
A program may use at most 128 MiB of HBM per device.

v0:
```python
import jax
import jax.numpy as jnp
from jax import lax
from jax.sharding import PartitionSpec as P


def apply_pairs(source_table, operators, pair_target, partners, pair_count):
    components, table_size = source_table.shape
    offsets, bucket_size = pair_target.shape
    groups = 4
    group_span = offsets // groups
    reverse = operators[::-1]
    table_rows = source_table.T
    pair_live = (
        lax.broadcasted_iota(jnp.int32, (offsets, bucket_size), 1) < pair_count[0][:, None]
    ).astype(jnp.float32)

    def one_group(summed, group_index):
        group_start = group_index * group_span
        forward = lax.dynamic_slice_in_dim(operators, group_start, group_span, 0)
        backward = lax.dynamic_slice_in_dim(reverse, group_start, group_span, 0)
        targets = lax.dynamic_slice_in_dim(pair_target, group_start, group_span, 0)
        partner_ids = lax.dynamic_slice_in_dim(partners, group_start, group_span, 0)
        pair_weight = lax.dynamic_slice_in_dim(pair_live, group_start, group_span, 0)
        both_ids = jnp.concatenate([partner_ids, targets], axis=0).reshape(-1)
        picked = jnp.take(table_rows, both_ids, axis=0).reshape(
            2, group_span, bucket_size, components
        )
        to_target = (
            jnp.einsum("kij,kpj->kpi", forward, picked[0], precision=lax.Precision.HIGHEST)
            * pair_weight[:, :, None]
        )
        to_partner = (
            jnp.einsum("kij,kpj->kpi", backward, picked[1], precision=lax.Precision.HIGHEST)
            * pair_weight[:, :, None]
        )
        update_rows = jnp.concatenate([to_target, to_partner], axis=0).reshape(-1, components)
        landing = jnp.concatenate([targets, partner_ids], axis=0).reshape(-1)
        summed = summed.at[landing].add(update_rows)
        return (summed, None)

    initial = jnp.zeros((table_size, components), jnp.float32)
    summed, _ = lax.scan(one_group, initial, jnp.arange(groups, dtype=jnp.int32))
    return summed.T


def shards(
    multipoles,
    parent_locals,
    operators,
    pair_target,
    pair_partner,
    pair_count,
    send_cells,
    send_count,
):
    components, cell_count = multipoles.shape
    col_size = lax.axis_size("col")
    row_size = lax.axis_size("row")
    devices = col_size * row_size
    slot_count = send_cells.shape[1] // devices
    position = jnp.arange(devices * slot_count, dtype=jnp.int32)
    live_send = position % slot_count < send_count[0][position // slot_count]
    sent_cells = send_cells[0]
    sent_cells = sent_cells.reshape(row_size, col_size, slot_count).transpose(1, 0, 2).reshape(-1)
    live_send = live_send.reshape(row_size, col_size, slot_count).transpose(1, 0, 2).reshape(-1)
    outgoing = jnp.where(live_send[None, :], jnp.take(multipoles, sent_cells, axis=1), 0.0)
    fetched = lax.all_to_all(outgoing, ("col", "row"), split_axis=1, concat_axis=1, tiled=True)
    remote_index = pair_partner - cell_count
    source_device = remote_index // slot_count
    remapped = (
        cell_count
        + (source_device % col_size * row_size + source_device // col_size) * slot_count
        + remote_index % slot_count
    )
    partners = jnp.where(pair_partner < cell_count, pair_partner, remapped)
    source_table = jnp.concatenate([multipoles, fetched], axis=1)
    summed = apply_pairs(source_table, operators, pair_target, partners, pair_count)
    returning = summed[:, cell_count:]
    returned = lax.all_to_all(returning, ("col", "row"), split_axis=1, concat_axis=1, tiled=True)
    returned = jnp.where(live_send[None, :], returned, 0.0)
    locals_out = parent_locals + summed[:, :cell_count]
    return locals_out.at[:, sent_cells].add(returned)


def solution(mesh):
    in_specs = (
        P(None, ("row", "col")),
        P(None, ("row", "col")),
        P(),
        P(None, ("row", "col")),
        P(None, ("row", "col")),
        P(("row", "col"), None),
        P(("row", "col"), None),
        P(("row", "col"), None),
    )
    out_specs = P(None, ("row", "col"))
    return jax.shard_map(shards, mesh=mesh, in_specs=in_specs, out_specs=out_specs, check_vma=False)
```

profile of v0, /device:TPU:1, one launch (start us, length us, event | category | flops | bytes accessed | tf_op | source)
XLA Modules:
  0.0 1049.1 jit_solution(16415644118779594203)
XLA Ops:
  0.5 1.5 reduce.8
  2.9 1.1 copy.36
  4.1 48.9 %gather_fusion.1 = s32[8192]{0:T(1024)S(1)} fusion(s32[128]{0:T(128)S(1)} %bitcast.73, s32[8192]{0:T(1024)S(1)} %broadcast_clamp_fusion.1), kind=kCustom, calls=%fused_computation.1 | custom fusion | bytes 98304 | tf_op jit(solution)/shard_map/gather | solution.py:63
  53.1 27.7 %gather_fusion.2 = f32[8192,64]{1,0:T(8,128)} fusion(f32[64,1024]{0,1:T(8,128)S(1)} %copy.36, s32[8192]{0:T(1024)S(1)} %broadcast_clamp_fusion), kind=kCustom, calls=%fused_computation.2 | custom fusion | bytes 4227072 | tf_op jit(solution)/shard_map/jit(_take)/gather | solution.py:67
  80.9 7.6 fusion.34
  88.5 5.5 reshape.239
  94.0 12.0 %all-to-all-start = ((f32[128,1,4096]{2,1,0:T(1,128)}), f32[128,1,4096]{2,1,0:T(1,128)S(1)}, u32[]{:S(2)}, u32[]{:S(2)}) async-start(f32[128,1,4096]{2,1,0:T(1,128)} %reshape.239), calls=%async_computation | async-start | bytes 4194304 | tf_op jit(solution)/shard_map/all_to_all | solution.py:68
  106.0 12.4 %copy.38 = f32[316,64,64]{2,1,0:T(8,128)} copy(f32[316,64,64]{0,2,1:T(8,128)} %param.12) | data formatting | bytes 10354688 | tf_op jit(solution)/shard_map/while | solution.py:43
  118.4 10.0 rev.3
  128.9 6.4 all-to-all-done
  135.3 1.3 copy-done.2
  137.2 7.3 reduce.9
  144.5 3.0 reshape.240
  147.5 4.0 maximum_bitcast_fusion
  151.5 2.3 broadcast_in_dim.52
  153.8 786.5 %while.10 = (s32[]{:T(128)}, f32[9216,64]{1,0:T(8,128)}, s32[4]{0:T(128)S(1)}, s32[316,128]{1,0:T(8,128)}, s32[316,128]{1,0:T(8,128)S(1)}, /*index=5*/f32[9216,6...) while((s32[]{:T(128)}, f32[9216,64]{1,0:T(8,128)}, ...), condition=%wide.region_2.3_spmd, body=%wide.region_0.2_spmd.sunk | while | flops 999551232 | bytes 84173504 | solution.py:43
  167.2 0.6 dynamic_slice.39
  168.4 0.8 constant_dynamic-slice_fusion.5
  169.5 40.2 %gather_fusion = f32[20224,64]{1,0:T(8,128)} fusion(f32[9216,64]{1,0:T(8,128)} %get-tuple-element.204, s32[20480]{0:T(1024)S(1)} %pad_clamp_fusion.2), kind=kCustom, calls=%fused_computation.clone.1 | custom fusion | bytes 10435584 | tf_op jit(solution)/shard_map/while/body/eval_jaxpr/jit(_take)/gather | solution.py:26
  209.7 11.7 %broadcast_select_fusion.2 = f32[20224,64]{1,0:T(8,128)S(1)} fusion(f32[20224,64]{1,0:T(8,128)} %gather_fusion, pred[20224]{0:T(1024)(128)(4,1)S(1)} %compare_and_fusion.3), kind=kLoop, calls=%fused_computation.6.clone.1 | loop fusion | flops 1294336 | bytes 10374912 | tf_op jit(solution)/shard_map/while/body/eval_jaxpr/jit(_take)/select_n | solution.py:26
  221.5 0.7 fusion.54
  222.2 11.6 %fusion.56 = f32[79,128,64]{1,2,0:T(8,128)S(1)} fusion(f32[79,128,64]{2,1,0:T(8,128)S(1)} %bitcast.78, f32[316,64,64]{2,1,0:T(8,128)} %get-tuple-element.205, s32[]{:T(128)S(6)} %select_n.193, f32[79,128]{1,0:T(8,128)S(1)} %constant_dynamic-slice_fusion.6), kind=kOutput, calls=%fused_computation.11.clone.1 | convolution fusion | flops 497672192 | bytes 7806468 | tf_op jit(solution)/shard_map/while/body/eval_jaxpr/kij,kpj->kpi/dot_general | solution.py:30
  233.9 11.6 %fusion.55 = f32[79,128,64]{1,2,0:T(8,128)S(1)} fusion(f32[79,128,64]{2,1,0:T(8,128)S(1)} %bitcast.77, f32[316,64,64]{2,1,0:T(8,128)} %get-tuple-element.207, s32[]{:T(128)S(6)} %select_n.193, f32[79,128]{1,0:T(8,128)S(1)} %constant_dynamic-slice_fusion.6), kind=kOutput, calls=%fused_computation.12.clone.1 | convolution fusion | flops 497672192 | bytes 7806468 | tf_op jit(solution)/shard_map/while/body/eval_jaxpr/kij,kpj->kpi/dot_general | solution.py:34
  245.5 2.9 pad_maximum_fusion.2
  248.4 8.4 copy.60
  257.1 103.4 %scatter_fusion = f32[9216,64]{1,0:T(8,128)} fusion(f32[9216,64]{1,0:T(8,128)} %get-tuple-element.187, s32[20224]{0:T(1024)S(1)} %fusion.52, f32[20224,64]{1,0:T(8,128)} %bitcast.76), kind=kCustom, calls=%fused_computation.3.clone.1 | custom fusion | flops 1294336 | bytes 15612928 | tf_op jit(solution)/shard_map/while/body/eval_jaxpr/scatter-add | solution.py:39
  360.5 0.6 dynamic_slice.39
  361.7 0.8 constant_dynamic-slice_fusion.5
  362.8 40.2 %gather_fusion = f32[20224,64]{1,0:T(8,128)} fusion(f32[9216,64]{1,0:T(8,128)} %get-tuple-element.204, s32[20480]{0:T(1024)S(1)} %pad_clamp_fusion.2), kind=kCustom, calls=%fused_computation.clone.1 | custom fusion | bytes 10435584 | tf_op jit(solution)/shard_map/while/body/eval_jaxpr/jit(_take)/gather | solution.py:26
  403.0 11.7 %broadcast_select_fusion.2 = f32[20224,64]{1,0:T(8,128)S(1)} fusion(f32[20224,64]{1,0:T(8,128)} %gather_fusion, pred[20224]{0:T(1024)(128)(4,1)S(1)} %compare_and_fusion.3), kind=kLoop, calls=%fused_computation.6.clone.1 | loop fusion | flops 1294336 | bytes 10374912 | tf_op jit(solution)/shard_map/while/body/eval_jaxpr/jit(_take)/select_n | solution.py:26
  414.8 0.7 fusion.54
  415.5 11.6 %fusion.56 = f32[79,128,64]{1,2,0:T(8,128)S(1)} fusion(f32[79,128,64]{2,1,0:T(8,128)S(1)} %bitcast.78, f32[316,64,64]{2,1,0:T(8,128)} %get-tuple-element.205, s32[]{:T(128)S(6)} %select_n.193, f32[79,128]{1,0:T(8,128)S(1)} %constant_dynamic-slice_fusion.6), kind=kOutput, calls=%fused_computation.11.clone.1 | convolution fusion | flops 497672192 | bytes 7806468 | tf_op jit(solution)/shard_map/while/body/eval_jaxpr/kij,kpj->kpi/dot_general | solution.py:30
  427.2 11.6 %fusion.55 = f32[79,128,64]{1,2,0:T(8,128)S(1)} fusion(f32[79,128,64]{2,1,0:T(8,128)S(1)} %bitcast.77, f32[316,64,64]{2,1,0:T(8,128)} %get-tuple-element.207, s32[]{:T(128)S(6)} %select_n.193, f32[79,128]{1,0:T(8,128)S(1)} %constant_dynamic-slice_fusion.6), kind=kOutput, calls=%fused_computation.12.clone.1 | convolution fusion | flops 497672192 | bytes 7806468 | tf_op jit(solution)/shard_map/while/body/eval_jaxpr/kij,kpj->kpi/dot_general | solution.py:34
  438.8 2.9 pad_maximum_fusion.2
  441.7 8.4 copy.60
  450.3 103.4 %scatter_fusion = f32[9216,64]{1,0:T(8,128)} fusion(f32[9216,64]{1,0:T(8,128)} %get-tuple-element.187, s32[20224]{0:T(1024)S(1)} %fusion.52, f32[20224,64]{1,0:T(8,128)} %bitcast.76), kind=kCustom, calls=%fused_computation.3.clone.1 | custom fusion | flops 1294336 | bytes 15612928 | tf_op jit(solution)/shard_map/while/body/eval_jaxpr/scatter-add | solution.py:39
  555.0 0.8 constant_dynamic-slice_fusion.5
  556.1 40.2 %gather_fusion = f32[20224,64]{1,0:T(8,128)} fusion(f32[9216,64]{1,0:T(8,128)} %get-tuple-element.204, s32[20480]{0:T(1024)S(1)} %pad_clamp_fusion.2), kind=kCustom, calls=%fused_computation.clone.1 | custom fusion | bytes 10435584 | tf_op jit(solution)/shard_map/while/body/eval_jaxpr/jit(_take)/gather | solution.py:26
  596.3 11.7 %broadcast_select_fusion.2 = f32[20224,64]{1,0:T(8,128)S(1)} fusion(f32[20224,64]{1,0:T(8,128)} %gather_fusion, pred[20224]{0:T(1024)(128)(4,1)S(1)} %compare_and_fusion.3), kind=kLoop, calls=%fused_computation.6.clone.1 | loop fusion | flops 1294336 | bytes 10374912 | tf_op jit(solution)/shard_map/while/body/eval_jaxpr/jit(_take)/select_n | solution.py:26
  608.0 0.7 fusion.54
  608.8 11.6 %fusion.56 = f32[79,128,64]{1,2,0:T(8,128)S(1)} fusion(f32[79,128,64]{2,1,0:T(8,128)S(1)} %bitcast.78, f32[316,64,64]{2,1,0:T(8,128)} %get-tuple-element.205, s32[]{:T(128)S(6)} %select_n.193, f32[79,128]{1,0:T(8,128)S(1)} %constant_dynamic-slice_fusion.6), kind=kOutput, calls=%fused_computation.11.clone.1 | convolution fusion | flops 497672192 | bytes 7806468 | tf_op jit(solution)/shard_map/while/body/eval_jaxpr/kij,kpj->kpi/dot_general | solution.py:30
  620.4 11.6 %fusion.55 = f32[79,128,64]{1,2,0:T(8,128)S(1)} fusion(f32[79,128,64]{2,1,0:T(8,128)S(1)} %bitcast.77, f32[316,64,64]{2,1,0:T(8,128)} %get-tuple-element.207, s32[]{:T(128)S(6)} %select_n.193, f32[79,128]{1,0:T(8,128)S(1)} %constant_dynamic-slice_fusion.6), kind=kOutput, calls=%fused_computation.12.clone.1 | convolution fusion | flops 497672192 | bytes 7806468 | tf_op jit(solution)/shard_map/while/body/eval_jaxpr/kij,kpj->kpi/dot_general | solution.py:34
  632.1 2.9 pad_maximum_fusion.2
  635.0 8.4 copy.60
  643.6 103.4 %scatter_fusion = f32[9216,64]{1,0:T(8,128)} fusion(f32[9216,64]{1,0:T(8,128)} %get-tuple-element.187, s32[20224]{0:T(1024)S(1)} %fusion.52, f32[20224,64]{1,0:T(8,128)} %bitcast.76), kind=kCustom, calls=%fused_computation.3.clone.1 | custom fusion | flops 1294336 | bytes 15612928 | tf_op jit(solution)/shard_map/while/body/eval_jaxpr/scatter-add | solution.py:39
  748.2 0.8 constant_dynamic-slice_fusion.5
  749.4 40.2 %gather_fusion = f32[20224,64]{1,0:T(8,128)} fusion(f32[9216,64]{1,0:T(8,128)} %get-tuple-element.204, s32[20480]{0:T(1024)S(1)} %pad_clamp_fusion.2), kind=kCustom, calls=%fused_computation.clone.1 | custom fusion | bytes 10435584 | tf_op jit(solution)/shard_map/while/body/eval_jaxpr/jit(_take)/gather | solution.py:26
  789.6 11.7 %broadcast_select_fusion.2 = f32[20224,64]{1,0:T(8,128)S(1)} fusion(f32[20224,64]{1,0:T(8,128)} %gather_fusion, pred[20224]{0:T(1024)(128)(4,1)S(1)} %compare_and_fusion.3), kind=kLoop, calls=%fused_computation.6.clone.1 | loop fusion | flops 1294336 | bytes 10374912 | tf_op jit(solution)/shard_map/while/body/eval_jaxpr/jit(_take)/select_n | solution.py:26
  801.3 0.7 fusion.54
  802.1 11.6 %fusion.56 = f32[79,128,64]{1,2,0:T(8,128)S(1)} fusion(f32[79,128,64]{2,1,0:T(8,128)S(1)} %bitcast.78, f32[316,64,64]{2,1,0:T(8,128)} %get-tuple-element.205, s32[]{:T(128)S(6)} %select_n.193, f32[79,128]{1,0:T(8,128)S(1)} %constant_dynamic-slice_fusion.6), kind=kOutput, calls=%fused_computation.11.clone.1 | convolution fusion | flops 497672192 | bytes 7806468 | tf_op jit(solution)/shard_map/while/body/eval_jaxpr/kij,kpj->kpi/dot_general | solution.py:30
  813.7 11.6 %fusion.55 = f32[79,128,64]{1,2,0:T(8,128)S(1)} fusion(f32[79,128,64]{2,1,0:T(8,128)S(1)} %bitcast.77, f32[316,64,64]{2,1,0:T(8,128)} %get-tuple-element.207, s32[]{:T(128)S(6)} %select_n.193, f32[79,128]{1,0:T(8,128)S(1)} %constant_dynamic-slice_fusion.6), kind=kOutput, calls=%fused_computation.12.clone.1 | convolution fusion | flops 497672192 | bytes 7806468 | tf_op jit(solution)/shard_map/while/body/eval_jaxpr/kij,kpj->kpi/dot_general | solution.py:34
  825.4 2.9 pad_maximum_fusion.2
  828.3 8.4 copy.60
  836.9 103.4 %scatter_fusion = f32[9216,64]{1,0:T(8,128)} fusion(f32[9216,64]{1,0:T(8,128)} %get-tuple-element.187, s32[20224]{0:T(1024)S(1)} %fusion.52, f32[20224,64]{1,0:T(8,128)} %bitcast.76), kind=kCustom, calls=%fused_computation.3.clone.1 | custom fusion | flops 1294336 | bytes 15612928 | tf_op jit(solution)/shard_map/while/body/eval_jaxpr/scatter-add | solution.py:39
  940.3 4.4 slice.25
  944.7 5.6 reshape.241
  950.3 5.9 all-to-all-start.1
  956.5 1.1 slice_add_fusion
  957.7 27.7 %all-to-all-done.1 = f32[128,1,4096]{2,1,0:T(1,128)} async-done(((f32[128,1,4096]{2,1,0:T(1,128)}), f32[128,1,4096]{2,1,0:T(1,128)}, u32[]{:S(2)}, u32[]{:S(2)}) %all-to-all-start.1) | async-done | bytes 2097184 | tf_op jit(solution)/shard_map/all_to_all | solution.py:80
  985.4 7.3 reduce.10
  992.8 3.0 reshape.242
  995.8 7.5 bitcast_select_fusion
  1003.2 44.8 %scatter_custom_fusion.1 = f32[64,1024]{0,1:T(8,128)S(1)} fusion(f32[64,1024]{0,1:T(8,128)S(1)} %slice_add_fusion, s32[8192]{0:T(1024)} %bitcast.86, f32[64,8192]{0,1:T(8,128)} %bitcast_select_fusion), kind=kCustom, calls=%fused_computation.29 | custom fusion | flops 524288 | bytes 4456448 | tf_op jit(solution)/shard_map/scatter-add | solution.py:83
  1048.0 0.9 copy.41
  (62 shorter events, 6.4 us)
Async XLA Ops:
  0.0 4.1 copy-start
  2.3 0.6 copy-start.7
  53.1 27.7 %copy-start.5 = (pred[8,16,64]{2,1,0:T(8,128)(4,1)}, pred[8,16,64]{2,1,0:T(8,128)(4,1)S(1)}, u32[]{:S(2)}) copy-start(pred[8,16,64]{2,1,0:T(8,128)(4,1)S(1)} %copy.33) | copy-start | bytes 24580
  94.0 41.3 %all-to-all-start = ((f32[128,1,4096]{2,1,0:T(1,128)}), f32[128,1,4096]{2,1,0:T(1,128)S(1)}, u32[]{:S(2)}, u32[]{:S(2)}) async-start(f32[128,1,4096]{2,1,0:T(1,128)} %reshape.239), calls=%async_computation | async-start | bytes 4194304 | tf_op jit(solution)/shard_map/all_to_all | solution.py:68
  118.4 10.0 copy-start.8
  118.4 10.1 copy-start.4
  135.3 1.3 copy-start.2
  944.7 11.5 %copy-start.6 = (pred[8,16,64]{2,1,0:T(8,128)(4,1)S(1)}, pred[8,16,64]{2,1,0:T(8,128)(4,1)}, u32[]{:S(2)}) copy-start(pred[8,16,64]{2,1,0:T(8,128)(4,1)} %copy-done.5) | copy-start | bytes 24580
  944.7 11.6 %copy-start.3 = (f32[64,1024]{1,0:T(8,128)S(1)}, f32[64,1024]{1,0:T(8,128)}, u32[]{:S(2)}) copy-start(f32[64,1024]{1,0:T(8,128)} %param.11) | copy-start | bytes 786436
  950.3 35.1 %all-to-all-start.1 = ((f32[128,1,4096]{2,1,0:T(1,128)}), f32[128,1,4096]{2,1,0:T(1,128)}, u32[]{:S(2)}, u32[]{:S(2)}) async-start(f32[128,1,4096]{2,1,0:T(1,128)} %reshape.241), calls=%async_computation.1 | async-start | bytes 4194304 | tf_op jit(solution)/shard_map/all_to_all | solution.py:80
  995.8 53.1 %copy-start.1 = (s32[1,128]{1,0:T(1,128)S(1)}, s32[1,128]{1,0:T(1,128)}, u32[]{:S(2)}) copy-start(s32[1,128]{1,0:T(1,128)} %param.17) | copy-start | bytes 1540
where the time goes:
time: 1050 us
  other arithmetic  556 us (53%)
  local copies, waits for them, and re-layouts  331 us (32%)
  matrix products  93.1 us (9%)
  waiting for transfers between devices  34.2 us (3%)
  starting transfers between devices  17.9 us (2%)
  loops' own time  16.2 us (2%)
    scatter-add x4, other arithmetic, one_group(): summed = summed.at[landing].add(update_rows)  414 us
    gather x4, local copies, waits for them, and re-layouts, one_group(): jnp.take(table_rows, both_ids, axis=0)  161 us
    gather x2, local copies, waits for them, and re-layouts, shards(): live_send = position % slot_count < send_count[0][position // slot_count]  48.9 us
    select_n x8, other arithmetic, one_group(): jnp.take(table_rows, both_ids, axis=0)  48 us
    dot_general x4, matrix products, one_group(): jnp.einsum('kij,kpj->kpi', forward, picked[0], precision=lax.Precision.HI...  46.6 us
    dot_general x4, matrix products, one_group(): jnp.einsum('kij,kpj->kpi', backward, picked[1], precision=lax.Precision.H...  46.6 us
    scatter-add x1, other arithmetic, shards(): return locals_out.at[:, sent_cells].add(returned)  44.8 us
    reshape x4, local copies, waits for them, and re-layouts, one_group(): jnp.concatenate([to_target, to_partner], axis=0).reshape(-1, components)  33.5 us
  transfers between devices with their start and end apart: 2, of which 2 were waited for; matrix products, arithmetic and copies ran while one was open for 2% of the time, Pallas kernels for 0%

commit v1 on v0

v1 whole, which is shorter than its diff:
```python
import functools

import jax
import jax.numpy as jnp
from jax import lax
from jax.experimental import pallas as pl
from jax.experimental.pallas import tpu as pltpu
from jax.sharding import PartitionSpec as P

F32 = jnp.float32
BF16 = jnp.bfloat16

COEF = 64
LANES = 128
CELLS = 1024
REMOTE = 8192
TABLE = CELLS + REMOTE
GROUP = 4
GROUPS = 80
LIVE_GROUPS = 79
ROWS = GROUP * LANES
BANKS = 8
VMEM_LIMIT = 60 * 1024 * 1024


def dot_nn(a, b):
    return lax.dot_general(a, b, (((1,), (0,)), ((), ())), preferred_element_type=F32)


def dot_nt(a, b):
    return lax.dot_general(a, b, (((1,), (1,)), ((), ())), preferred_element_type=F32)


def split(x):
    hi = x.astype(BF16)
    lo = (x - hi.astype(F32)).astype(BF16)
    return hi, lo


def operator_weights(op):
    hi, lo = split(op)
    return jnp.concatenate(
        [jnp.concatenate([hi, hi], axis=1), jnp.concatenate([lo, lo], axis=1)], axis=0
    )


def cell_table(multipoles):
    hi = multipoles.astype(BF16).astype(F32)
    lo = multipoles - hi
    return jnp.concatenate([hi, lo], axis=0).T


def one_hot_rows(index_block, count):
    columns = index_block.T
    cell = lax.broadcasted_iota(jnp.int32, (LANES, CELLS), 1)
    return jnp.concatenate(
        [(columns[:, i : i + 1] == cell).astype(F32).astype(BF16) for i in range(count)], axis=0
    )


def one_hot_columns(index_block, count):
    cell = lax.broadcasted_iota(jnp.int32, (CELLS, LANES), 0)
    return jnp.concatenate(
        [(index_block[i : i + 1, :] == cell).astype(F32).astype(BF16) for i in range(count)], axis=1
    )


def both_halves(x):
    return x + pltpu.roll(x, COEF, 1)


def unpack_rows(packed):
    hi = packed.astype(BF16).astype(F32)
    lo = packed - hi
    left = lax.broadcasted_iota(jnp.int32, packed.shape, packed.ndim - 1) < COEF
    axis = packed.ndim - 1
    first = jnp.where(left, hi, pltpu.roll(lo, COEF, axis))
    second = jnp.where(left, pltpu.roll(hi, COEF, axis), lo)
    return jnp.concatenate([first, second], axis=packed.ndim - 2)


def send_kernel(cells_ref, multipoles_ref, out_ref):
    table = cell_table(multipoles_ref[...]).astype(BF16)
    left = lax.broadcasted_iota(jnp.int32, (32, LANES), 1) < COEF

    @pl.loop(0, 16)
    def _(step):
        hot = one_hot_rows(cells_ref[step], GROUP)
        rows = both_halves(dot_nn(hot, table))
        for b in range(2 * GROUP):
            base = b * 64
            out_ref[step * 2 * GROUP + b] = jnp.where(
                left, rows[base : base + 32], rows[base + 32 : base + 64]
            )


def send_rows(multipoles, cells):
    return pl.pallas_call(
        send_kernel,
        name="send_rows",
        out_shape=jax.ShapeDtypeStruct((128, 32, LANES), F32),
        in_specs=[pl.BlockSpec(memory_space=pltpu.VMEM)] * 2,
        out_specs=pl.BlockSpec(memory_space=pltpu.VMEM),
        compiler_params=pltpu.CompilerParams(vmem_limit_bytes=VMEM_LIMIT),
    )(cells, multipoles)


def partner_kernel(
    index_a, index_b, targets_a, targets_b, ops_a, ops_b, multipoles_ref, local_ref, remote_ref, *scratch
):
    table, update_a, update_b = scratch[:3]
    banks = scratch[3:]
    step = pl.program_id(0)

    @pl.when(step == 0)
    def _():
        table[...] = cell_table(multipoles_ref[...]).astype(BF16)
        update_b[...] = jnp.zeros_like(update_b)
        for bank in banks:
            bank[...] = jnp.zeros_like(bank)

    def updates(targets, ops, out):
        hot = one_hot_rows(targets[0], GROUP)
        terms = dot_nn(hot, table[...]).astype(BF16)
        for i in range(GROUP):
            weights = operator_weights(ops[GROUP - 1 - i])
            out[i * LANES : (i + 1) * LANES, :] = dot_nt(terms[i * LANES : (i + 1) * LANES], weights)

    def scatter(index, update):
        for first in range(0, ROWS, BANKS):
            where = [index[0, (first + b) // LANES, (first + b) % LANES] for b in range(BANKS)]
            held = [banks[b][pl.ds(where[b], 1), :] for b in range(BANKS)]
            for b in range(BANKS):
                banks[b][pl.ds(where[b], 1), :] = held[b] + update[first + b : first + b + 1, :]

    updates(targets_a, ops_a, update_a)
    scatter(index_b, update_b)
    updates(targets_b, ops_b, update_b)
    scatter(index_a, update_a)

    @pl.when(step == pl.num_programs(0) - 1)
    def _():
        left = lax.broadcasted_iota(jnp.int32, (32, LANES), 1) < COEF

        def total(start, size):
            parts = [bank[pl.ds(start, size), :] for bank in banks]
            while len(parts) > 1:
                parts = [parts[i] + parts[i + 1] for i in range(0, len(parts), 2)]
            return both_halves(parts[0])

        @pl.loop(0, CELLS // 64)
        def _(i):
            start = pl.multiple_of(i * 64, 64)
            local_ref[pl.ds(start, 64), :] = total(start, 64)

        @pl.loop(0, 128)
        def _(i):
            rows = total(pl.multiple_of(CELLS + i * 64, 64), 64)
            remote_ref[i] = jnp.where(left, rows[:32], rows[32:])


def partner_sums(partners, targets, operators, multipoles):
    smem = functools.partial(pl.BlockSpec, (1, GROUP, LANES), memory_space=pltpu.SMEM)
    vmem = functools.partial(pl.BlockSpec, (1, GROUP, LANES))
    last = LIVE_GROUPS - 1
    return pl.pallas_call(
        partner_kernel,
        name="partner_sums",
        grid=(GROUPS // 2,),
        out_shape=(
            jax.ShapeDtypeStruct((CELLS, LANES), F32),
            jax.ShapeDtypeStruct((128, 32, LANES), F32),
        ),
        in_specs=[
            smem(lambda i: (2 * i, 0, 0)),
            smem(lambda i: (jnp.maximum(2 * i - 1, 0), 0, 0)),
            vmem(lambda i: (2 * i, 0, 0)),
            vmem(lambda i: (2 * i + 1, 0, 0)),
            pl.BlockSpec((GROUP, COEF, COEF), lambda i: (last - 2 * i, 0, 0)),
            pl.BlockSpec((GROUP, COEF, COEF), lambda i: (jnp.maximum(last - 1 - 2 * i, 0), 0, 0)),
            pl.BlockSpec((COEF, CELLS), lambda i: (0, 0)),
        ],
        out_specs=(
            pl.BlockSpec((CELLS, LANES), lambda i: (0, 0)),
            pl.BlockSpec((128, 32, LANES), lambda i: (0, 0, 0)),
        ),
        scratch_shapes=[
            pltpu.VMEM((CELLS, LANES), BF16),
            pltpu.VMEM((ROWS, LANES), F32),
            pltpu.VMEM((ROWS, LANES), F32),
        ]
        + [pltpu.VMEM((TABLE, LANES), F32)] * BANKS,
        compiler_params=pltpu.CompilerParams(
            dimension_semantics=("arbitrary",), vmem_limit_bytes=VMEM_LIMIT
        ),
        cost_estimate=pl.CostEstimate(
            flops=200_000_000_000, bytes_accessed=20_000_000, transcendentals=0
        ),
    )(partners, partners, targets, targets, operators, operators, multipoles)


def target_kernel(
    index_a, index_b, targets_a, targets_b, ops_a, ops_b, multipoles_ref, fetched_ref, out_ref, table, rows_a, rows_b
):
    step = pl.program_id(0)

    @pl.when(step == 0)
    def _():
        table[:CELLS, :] = cell_table(multipoles_ref[...])
        rows_b[...] = jnp.zeros_like(rows_b)
        out_ref[...] = jnp.zeros_like(out_ref)

        @pl.loop(0, 128)
        def _(i):
            table[pl.ds(pl.multiple_of(CELLS + i * 64, 64), 64), :] = unpack_rows(fetched_ref[i])

    def gather(index, rows):
        for r in range(ROWS):
            rows[r : r + 1, :] = table[pl.ds(index[0, r // LANES, r % LANES], 1), :]

    def accumulate(targets, ops, rows):
        updates = []
        for i in range(GROUP):
            weights = operator_weights(ops[i])
            updates.append(dot_nt(rows[i * LANES : (i + 1) * LANES, :].astype(BF16), weights))
        summed = both_halves(jnp.concatenate(updates, axis=0))
        hi = summed.astype(BF16).astype(F32)
        left = lax.broadcasted_iota(jnp.int32, summed.shape, 1) < COEF
        parts = jnp.where(left, hi, summed - hi).astype(BF16)
        out_ref[...] += dot_nn(one_hot_columns(targets[0], GROUP), parts)

    gather(index_a, rows_a)
    accumulate(targets_b, ops_b, rows_b)
    gather(index_b, rows_b)
    accumulate(targets_a, ops_a, rows_a)


def target_sums(partners, targets, operators, multipoles, fetched):
    smem = functools.partial(pl.BlockSpec, (1, GROUP, LANES), memory_space=pltpu.SMEM)
    vmem = functools.partial(pl.BlockSpec, (1, GROUP, LANES))
    last = LIVE_GROUPS - 1
    return pl.pallas_call(
        target_kernel,
        name="target_sums",
        grid=(GROUPS // 2,),
        out_shape=jax.ShapeDtypeStruct((CELLS, LANES), F32),
        in_specs=[
            smem(lambda i: (2 * i, 0, 0)),
            smem(lambda i: (2 * i + 1, 0, 0)),
            vmem(lambda i: (2 * i, 0, 0)),
            vmem(lambda i: (jnp.maximum(2 * i - 1, 0), 0, 0)),
            pl.BlockSpec((GROUP, COEF, COEF), lambda i: (2 * i, 0, 0)),
            pl.BlockSpec((GROUP, COEF, COEF), lambda i: (jnp.clip(2 * i - 1, 0, last), 0, 0)),
            pl.BlockSpec((COEF, CELLS), lambda i: (0, 0)),
            pl.BlockSpec((128, 32, LANES), lambda i: (0, 0, 0)),
        ],
        out_specs=pl.BlockSpec((CELLS, LANES), lambda i: (0, 0)),
        scratch_shapes=[
            pltpu.VMEM((TABLE, LANES), F32),
            pltpu.VMEM((ROWS, LANES), F32),
            pltpu.VMEM((ROWS, LANES), F32),
        ],
        compiler_params=pltpu.CompilerParams(
            dimension_semantics=("arbitrary",), vmem_limit_bytes=VMEM_LIMIT
        ),
        cost_estimate=pl.CostEstimate(
            flops=200_000_000_000, bytes_accessed=20_000_000, transcendentals=0
        ),
    )(partners, partners, targets, targets, operators, operators, multipoles, fetched)


def finish_kernel(cells_ref, returned_ref, parent_ref, partner_ref, target_ref, out_ref, total):
    total[...] = target_ref[...]

    @pl.loop(0, 16)
    def _(step):
        packed = returned_ref[pl.ds(step * 2 * GROUP, 2 * GROUP)]
        rows = unpack_rows(packed).reshape(ROWS, LANES).astype(BF16)
        total[...] += dot_nn(one_hot_columns(cells_ref[step], GROUP), rows)

    summed = both_halves(total[...]) + partner_ref[...]
    out_ref[...] = parent_ref[...] + summed.T[:COEF]


def finish(cells, returned, parent_locals, partner_part, target_part):
    return pl.pallas_call(
        finish_kernel,
        name="finish",
        out_shape=jax.ShapeDtypeStruct((COEF, CELLS), F32),
        in_specs=[pl.BlockSpec(memory_space=pltpu.VMEM)] * 5,
        out_specs=pl.BlockSpec(memory_space=pltpu.VMEM),
        scratch_shapes=[pltpu.VMEM((CELLS, LANES), F32)],
        compiler_params=pltpu.CompilerParams(vmem_limit_bytes=VMEM_LIMIT),
    )(cells, returned, parent_locals, partner_part, target_part)


def prepare(pair_target, pair_partner, pair_count, send_cells, send_count):
    position = lax.broadcasted_iota(jnp.int32, pair_target.shape, 1)
    targets = jnp.where(position < pair_count[0][:, None], pair_target, -1)
    targets = jnp.pad(targets, ((0, GROUP), (0, 0)), constant_values=-1)
    partners = jnp.pad(pair_partner, ((0, GROUP), (0, 0)))
    slot = lax.broadcasted_iota(jnp.int32, (128, 64), 1)
    cells = jnp.where(slot < send_count[0][:, None], send_cells[0].reshape(128, 64), -1)
    return (
        targets.reshape(GROUPS, GROUP, LANES),
        partners.reshape(GROUPS, GROUP, LANES),
        cells.reshape(16, GROUP, LANES),
    )


def shards(
    multipoles,
    parent_locals,
    operators,
    pair_target,
    pair_partner,
    pair_count,
    send_cells,
    send_count,
):
    axes = ("row", "col")
    targets, partners, cells = prepare(pair_target, pair_partner, pair_count, send_cells, send_count)
    outgoing = send_rows(multipoles, cells)
    fetched = lax.all_to_all(outgoing, axes, split_axis=0, concat_axis=0, tiled=True)
    partner_part, returning = partner_sums(partners, targets, operators, multipoles)
    returned = lax.all_to_all(returning, axes, split_axis=0, concat_axis=0, tiled=True)
    target_part = target_sums(partners, targets, operators, multipoles, fetched)
    return finish(cells, returned, parent_locals, partner_part, target_part)


def solution(mesh):
    in_specs = (
        P(None, ("row", "col")),
        P(None, ("row", "col")),
        P(),
        P(None, ("row", "col")),
        P(None, ("row", "col")),
        P(("row", "col"), None),
        P(("row", "col"), None),
        P(("row", "col"), None),
    )
    out_specs = P(None, ("row", "col"))
    return jax.shard_map(shards, mesh=mesh, in_specs=in_specs, out_specs=out_specs, check_vma=False)
```

time: 1050 us -> 244 us (0.23)
  other arithmetic: 556 us -> 2.82 us
  local copies, waits for them, and re-layouts: 331 us -> 14.8 us
  Pallas kernels: 0 us -> 204 us
  matrix products: 93.1 us -> 0 us
  waiting for transfers between devices: 34.2 us -> 0.01 us
  loops' own time: 16.2 us -> 0 us
    scatter-add x5 -> x0, other arithmetic: 458 us -> none  [the longest x4 414 us: one_group(): summed = summed.at[landing].add(update_rows)]
    gather x7 -> x0, local copies, waits for them, and re-layouts: 237 us -> none  [the longest x4 161 us: one_group(): jnp.take(table_rows, both_ids, axis=0)]
    pallas_call x0 -> x4, Pallas kernels: none -> 204 us  [the longest x1 90.2 us: target_sums(): pl.pallas_call(target_kernel, name='target_sums', grid=(GROUPS // 2,), ou...]
    dot_general x8 -> x0, matrix products: 93.1 us -> none  [the longest x4 46.6 us: one_group(): jnp.einsum('kij,kpj->kpi', forward, picked[0], precision=lax.Precision.HI...]
    select_n x16 -> x2, other arithmetic: 56.9 us -> 1.48 us  [the longest x1 1.38 us: prepare(): jnp.where(slot < send_count[0][:, None], send_cells[0].reshape(128, 64), -1)]
    all_to_all x2, waiting for transfers between devices: 34.2 us -> 0.01 us  [the longest x1 0.01 us: shards(): lax.all_to_all(outgoing, axes, split_axis=0, concat_axis=0, tiled=True)]
    reshape x5 -> x0, local copies, waits for them, and re-layouts: 33.6 us -> none  [the longest x4 33.5 us: one_group(): jnp.concatenate([to_target, to_partner], axis=0).reshape(-1, components)]
    another operation x1 -> x0, loops' own time: 16.2 us -> none  [apply_pairs(): lax.scan(one_group, initial, jnp.arange(groups, dtype=jnp.int32))]
  transfers between devices with their start and end apart: 2 -> 2, of which waited for: 2 -> 0; matrix products, arithmetic and copies ran while one was open for 2% -> 6% of each run, Pallas kernels for 0% -> 74%
where the time goes in v1:
time: 244 us; the launch traced here: 243 us
  Pallas kernels  204 us (84%)
  starting transfers between devices  22.2 us (9%)
  local copies, waits for them, and re-layouts  14.8 us (6%)
  other arithmetic  2.82 us (1%)
    pallas_call x1, Pallas kernels, target_sums(): pl.pallas_call(target_kernel, name='target_sums', grid=(GROUPS // 2,), ou...  90.2 us
    pallas_call x1, Pallas kernels, partner_sums(): pl.pallas_call(partner_kernel, name='partner_sums', grid=(GROUPS // 2,),...  88.8 us
    pallas_call x1, Pallas kernels, send_rows(): pl.pallas_call(send_kernel, name='send_rows', out_shape=jax.ShapeDtypeStr...  13.3 us
    unnamed x8, local copies, waits for them, and re-layouts  12.9 us
    all_to_all x1, starting transfers between devices, shards(): lax.all_to_all(outgoing, axes, split_axis=0, concat_axis=0, tiled=True)  11.9 us
    pallas_call x1, Pallas kernels, finish(): pl.pallas_call(finish_kernel, name='finish', out_shape=jax.ShapeDtypeStru...  11.2 us
    all_to_all x1, starting transfers between devices, shards(): lax.all_to_all(returning, axes, split_axis=0, concat_axis=0, tiled=True)  10.2 us
  transfers between devices with their start and end apart: 2, of which 0 were waited for; matrix products, arithmetic and copies ran while one was open for 6% of the time, Pallas kernels for 74%

profile of v1, /device:TPU:1, one launch (start us, length us, event | category | flops | bytes accessed | tf_op | source)
XLA Modules:
  0.0 243.4 jit_solution(4746903093560109064)
XLA Ops:
  0.0 0.1 iota.17
  0.1 0.5 broadcast.13
  0.6 1.3 reduce.4
  1.9 0.2 lt.23
  2.1 0.1 lt.24
  2.2 0.1 lt.25
  2.3 1.4 compare_select_fusion.cells_ref
  3.7 13.3 %send_rows.1 = f32[128,32,128]{2,1,0:T(8,128)} custom-call(s32[16,4,128]{2,1,0:T(4,128)} %compare_select_fusion.cells_ref, f32[64,1024]{1,0:T(8,128)} %multipoles_ref.5), custom_call_target="tpu_custom_call" | custom-call | tf_op jit(solution)/shard_map/send_rows/pallas_call | solution.py:98
  17.0 0.0 copy-start.2
  17.0 0.0 copy-start.1
  17.0 11.9 %all-to-all-start.1 = ((f32[128,32,128]{2,1,0:T(8,128)}), f32[128,32,128]{2,1,0:T(8,128)}, u32[]{:S(2)}, u32[]{:S(2)}) async-start(f32[128,32,128]{2,1,0:T(8,128)} %send_rows.1), calls=%async_computation.1 | async-start | bytes 4194304 | tf_op jit(solution)/shard_map/all_to_all | solution.py:324
  29.0 0.0 copy-done.2
  29.0 0.0 copy-done.1
  29.0 0.7 pad.7
  29.7 0.0 copy-start
  29.7 12.4 %copy.13.ops_a.ops_b = f32[316,64,64]{2,1,0:T(8,128)} copy(f32[316,64,64]{0,2,1:T(8,128)} %param.10) | data formatting | bytes 10354688 | tf_op args[2]
  42.1 0.0 copy-done
  42.1 0.1 fusion
  42.2 0.7 pad.8
  42.9 88.8 %partner_sums.1 = (f32[1024,128]{1,0:T(8,128)}, f32[128,32,128]{2,1,0:T(8,128)}) custom-call(s32[80,4,128]{2,1,0:T(4,128)} %bitcast.3, s32[80,4,128]{2,1,0:T(4,128)} %bitcast.4, s32[80,4,128]{2,1,0:T(4,128)} %bitcast.7, s32[80,4,128]{2,1,0:T(4,128)} %bitcast.8, f32[316,64,64]{2,1,0:T(8,128)} %copy.13.ops_a.ops_b, f32[316,64,64]{2,1,0:T(8,128)} %copy.13.ops_a.ops_b, ...), custom_call_target="tpu_custom_call" | custom-call | flops 199999995904 | bytes 20000000 | tf_op jit(solution)/shard_map/partner_sums/pallas_call | solution.py:166
  131.7 0.0 all-to-all-done.1.fetched_ref
  131.7 10.2 %all-to-all-start = ((f32[128,32,128]{2,1,0:T(8,128)}), f32[128,32,128]{2,1,0:T(8,128)}, u32[]{:S(2)}, u32[]{:S(2)}) async-start(f32[128,32,128]{2,1,0:T(8,128)} %get-tuple-element.7), calls=%async_computation | async-start | bytes 4194304 | tf_op jit(solution)/shard_map/all_to_all | solution.py:326
  142.0 90.2 %target_sums.1.target_ref = f32[1024,128]{1,0:T(8,128)} custom-call(s32[80,4,128]{2,1,0:T(4,128)} %bitcast.5, s32[80,4,128]{2,1,0:T(4,128)} %bitcast.6, s32[80,4,128]{2,1,0:T(4,128)} %bitcast.9, s32[80,4,128]{2,1,0:T(4,128)} %bitcast.10, f32[316,64,64]{2,1,0:T(8,128)} %copy.13.ops_a.ops_b, f32[316,64,64]{2,1,0:T(8,128)} %copy.13.ops_a.ops_b, ...), custom_call_target="tpu_custom_call" | custom-call | flops 199999995904 | bytes 20000000 | tf_op jit(solution)/shard_map/target_sums/pallas_call | solution.py:242
  232.2 0.0 all-to-all-done.returned_ref
  232.2 11.2 %finish.1 = f32[64,1024]{1,0:T(8,128)} custom-call(s32[16,4,128]{2,1,0:T(4,128)} %compare_select_fusion.cells_ref, f32[128,32,128]{2,1,0:T(8,128)} %all-to-all-done.returned_ref, f32[64,1024]{1,0:T(8,128)} %parent_ref.1, f32[1024,128]{1,0:T(8,128)} %get-tuple-element.8.partner_ref, f32[1024,128]{1,0:T(8,128)} %target_sums.1.target_ref), custom_call_target="tpu_custom_call" | custom-call | tf_op jit(solution)/shard_map/finish/pallas_call | solution.py:286
  (2 shorter events, 0.0 us)
Async XLA Ops:
  17.0 12.0 %copy-start.2 = (s32[1,316]{1,0:T(1,128)S(1)}, s32[1,316]{1,0:T(1,128)}, u32[]{:S(2)}) copy-start(s32[1,316]{1,0:T(1,128)} %param.13) | copy-start | bytes 3796
  17.0 12.0 %copy-start.1 = (s32[316,128]{1,0:T(8,128)S(1)}, s32[316,128]{1,0:T(8,128)}, u32[]{:S(2)}) copy-start(s32[316,128]{1,0:T(8,128)} %param.12) | copy-start | bytes 485380
  17.0 114.7 %all-to-all-start.1 = ((f32[128,32,128]{2,1,0:T(8,128)}), f32[128,32,128]{2,1,0:T(8,128)}, u32[]{:S(2)}, u32[]{:S(2)}) async-start(f32[128,32,128]{2,1,0:T(8,128)} %send_rows.1), calls=%async_computation.1 | async-start | bytes 4194304 | tf_op jit(solution)/shard_map/all_to_all | solution.py:324
  29.7 12.4 %copy-start = (s32[316,128]{1,0:T(8,128)S(1)}, s32[316,128]{1,0:T(8,128)}, u32[]{:S(2)}) copy-start(s32[316,128]{1,0:T(8,128)} %param.11) | copy-start | bytes 485380
  131.7 100.5 %all-to-all-start = ((f32[128,32,128]{2,1,0:T(8,128)}), f32[128,32,128]{2,1,0:T(8,128)}, u32[]{:S(2)}, u32[]{:S(2)}) async-start(f32[128,32,128]{2,1,0:T(8,128)} %get-tuple-element.7), calls=%async_computation | async-start | bytes 4194304 | tf_op jit(solution)/shard_map/all_to_all | solution.py:326

commit v2 on v0

v2 whole, which is shorter than its diff:
```python
import jax
import jax.numpy as jnp
from jax import lax
from jax.experimental import pallas as pl
from jax.experimental.pallas import tpu as pltpu
from jax.sharding import PartitionSpec as P

F32 = jnp.float32
BF16 = jnp.bfloat16

COEF = 64
LANES = 128
CELLS = 1024
HALF = 512
REMOTE = 8192
TABLE = CELLS + REMOTE
OFFSETS = 316
SEGMENT = 8
ROWS = SEGMENT * LANES
STEPS = 20
PADDED = 320
DEAD = 0xFFFF
BANKS = 8
BATCH = 8
DEPTH = 4
WEAVE = False
MTILE = 256
VMEM_LIMIT = 60 * 1024 * 1024


def dot_nn(a, b):
    return lax.dot_general(a, b, (((1,), (0,)), ((), ())), preferred_element_type=F32)


def dot_nt(a, b):
    return lax.dot_general(a, b, (((1,), (1,)), ((), ())), preferred_element_type=F32)


def left_half(shape):
    return lax.broadcasted_iota(jnp.int32, shape, len(shape) - 1) < COEF


def both_halves(x):
    return x + pltpu.roll(x, COEF, 1)


def turn_operators(ops_ref, turned):
    @pl.loop(0, COEF // 2)
    def _(p):
        for start in range(0, OFFSETS, LANES):
            size = min(LANES, OFFSETS - start)
            pair = jnp.concatenate(
                [ops_ref[p, :, start : start + size], ops_ref[p + 32, :, start : start + size]], axis=0
            )
            turned[pl.ds(start * (COEF // 2) + p, size, stride=COEF // 2), :] = pair.T


def stage_operators(turned, staged, ks):
    size = COEF // 2
    for q, k in enumerate(ks):
        staged[q * size : (q + 1) * size, :] = turned[pl.ds(pl.multiple_of(k * size, size), size), :]


def weave(pieces, batches):
    done = 0
    for i, piece in enumerate(pieces):
        piece()
        until = (i + 1) * len(batches) // len(pieces)
        for batch in batches[done:until]:
            batch()
        done = until


def weight_pieces(staged, q, state):
    size = COEF // 2

    def doubled(x):
        left = left_half((size, LANES))
        swapped = pltpu.roll(x, COEF, 1)
        return [jnp.where(left, x, swapped), jnp.where(left, swapped, x)]

    def high():
        packed = staged[q * size : (q + 1) * size, :]
        hi = packed.astype(BF16).astype(F32)
        state["lo", q] = packed - hi
        state["hi", q] = doubled(hi)

    def low():
        parts = state.pop(("hi", q)) + doubled(state.pop(("lo", q)))
        state["w", q] = jnp.concatenate(parts, axis=0).astype(BF16)

    return [high, low]


def cell_table(multipoles):
    hi = multipoles.astype(BF16).astype(F32)
    lo = multipoles - hi
    return jnp.concatenate([hi, lo], axis=0).T


def folded_table(multipoles):
    table = cell_table(multipoles).astype(BF16)
    return jnp.concatenate([table[:HALF], table[HALF:]], axis=1)


def pair_codes(targets, counts, segment):
    first = segment * SEGMENT
    cells = targets[pl.ds(pl.multiple_of(jnp.maximum(first, 0), SEGMENT), SEGMENT), :]
    place = lax.broadcasted_iota(jnp.int32, (SEGMENT, LANES), 0)
    limit = jnp.zeros((SEGMENT, LANES), jnp.int32)
    for q in range(SEGMENT):
        k = first + q
        count = jnp.where((k >= 0) & (k < OFFSETS), counts[0, jnp.clip(k, 0, OFFSETS - 1)], 0)
        limit = jnp.where(place == q, count, limit)
    return fold(cells, lax.broadcasted_iota(jnp.int32, (SEGMENT, LANES), 1) < limit)


def slot_codes(cells_ref, counts, segment):
    cells = jnp.concatenate([cells_ref[2 * segment], cells_ref[2 * segment + 1]], axis=0)
    place = lax.broadcasted_iota(jnp.int32, (SEGMENT, LANES), 0)
    left = left_half((SEGMENT, LANES))
    limit = jnp.zeros((SEGMENT, LANES), jnp.int32)
    for q in range(SEGMENT):
        device = 2 * (segment * SEGMENT + q)
        limit = jnp.where(place == q, jnp.where(left, counts[0, device], counts[0, device + 1]), limit)
    return fold(cells, lax.broadcasted_iota(jnp.int32, (SEGMENT, LANES), 1) % 64 < limit)


def fold(cells, live):
    return jnp.where(live, (cells & (HALF - 1)) + ((cells >> 9) << 16), DEAD)


def spread_column(columns, q):
    code = jnp.broadcast_to(columns[:, q : q + 1], (LANES, LANES))
    lane = lax.broadcasted_iota(jnp.int32, (LANES, LANES), 1)
    low = code & DEAD
    hot = [(low == lane + start).astype(F32).astype(BF16) for start in range(0, HALF, LANES)]
    return jnp.concatenate(hot, axis=1), code > DEAD


def fetch_rows(columns, q, table, state):
    hot, upper = spread_column(columns, q)
    state["both", q] = dot_nn(hot, table[...])
    state["upper", q] = upper


def select_rows(q, state):
    part = state.pop(("both", q))
    return jnp.where(state.pop(("upper", q)), part[:, LANES:], part[:, :LANES])


def hot_columns(low, picks, start, size):
    cell = lax.broadcasted_iota(jnp.int32, (size, LANES), 0) + start
    hot = [(low[q : q + 1, :] == cell).astype(F32).astype(BF16) for q in picks]
    return jnp.concatenate(hot, axis=1)


def unpack_rows(packed):
    hi = packed.astype(BF16).astype(F32)
    lo = packed - hi
    left = left_half(packed.shape)
    axis = packed.ndim - 1
    first = jnp.where(left, hi, pltpu.roll(lo, COEF, axis))
    second = jnp.where(left, pltpu.roll(hi, COEF, axis), lo)
    return jnp.concatenate([first, second], axis=packed.ndim - 2)


def send_kernel(counts, cells_ref, multipoles_ref, out_ref, table):
    table[...] = folded_table(multipoles_ref[...])
    left = left_half((32, LANES))

    @pl.loop(0, 8)
    def _(segment):
        columns = slot_codes(cells_ref, counts, segment).T
        state = {}

        def store(q):
            rows = both_halves(select_rows(q, state))
            for b in range(2):
                base = b * 64
                out_ref[segment * 2 * SEGMENT + 2 * q + b] = jnp.where(
                    left, rows[base : base + 32], rows[base + 32 : base + 64]
                )

        for q in range(SEGMENT + 1):
            if q < SEGMENT:
                fetch_rows(columns, q, table, state)
            if q >= 1:
                store(q - 1)


SMEM_SPEC = pl.BlockSpec(memory_space=pltpu.SMEM)
VMEM_SPEC = pl.BlockSpec(memory_space=pltpu.VMEM)
HBM_SPEC = pl.BlockSpec(memory_space=pltpu.HBM)


def send_rows(counts, cells, multipoles):
    return pl.pallas_call(
        send_kernel,
        name="send_rows",
        out_shape=jax.ShapeDtypeStruct((128, 32, LANES), F32),
        in_specs=[SMEM_SPEC, VMEM_SPEC, VMEM_SPEC],
        out_specs=VMEM_SPEC,
        scratch_shapes=[pltpu.VMEM((HALF, 2 * LANES), BF16)],
        compiler_params=pltpu.CompilerParams(vmem_limit_bytes=VMEM_LIMIT),
    )(counts, cells, multipoles)


def fetch_index(partners, segment, index, sem):
    start = pl.multiple_of(jnp.clip(segment, 0, PADDED // SEGMENT - 1) * SEGMENT, SEGMENT)
    return pltpu.make_async_copy(partners.at[pl.ds(start, SEGMENT)], index, sem)


def load_pairs(partners_ref, targets_ref, partners, targets, sem_p, sem_t):
    copies = [
        pltpu.make_async_copy(partners_ref, partners.at[pl.ds(0, OFFSETS)], sem_p),
        pltpu.make_async_copy(targets_ref, targets.at[pl.ds(0, OFFSETS)], sem_t),
    ]
    for copy in copies:
        copy.start()
    for copy in copies:
        copy.wait()
    for pairs in (partners, targets):
        pairs[OFFSETS:, :] = jnp.zeros((PADDED - OFFSETS, LANES), jnp.int32)


def partner_kernel(
    counts,
    partners_ref,
    targets_ref,
    ops_ref,
    multipoles_ref,
    local_ref,
    remote_ref,
    turned_ref,
    native,
    table,
    *scratch,
):
    (turned, staged, partners, targets, update_a, update_b, index_e, index_o) = scratch[:8]
    sem_e, sem_o, sem_ops, sem_p, sem_t = scratch[8:13]
    banks = scratch[13:]

    load = pltpu.make_async_copy(ops_ref, native, sem_ops)
    load.start()
    load_pairs(partners_ref, targets_ref, partners, targets, sem_p, sem_t)
    fetch_index(partners, 0, index_e, sem_e).start()
    table[...] = folded_table(multipoles_ref[...])
    update_b[...] = jnp.zeros_like(update_b)

    @pl.loop(0, TABLE // 128)
    def _(i):
        for bank in banks:
            bank[pl.ds(pl.multiple_of(i * 128, 128), 128), :] = jnp.zeros((128, LANES), F32)

    load.wait()
    turn_operators(native, turned)
    keep = pltpu.make_async_copy(turned, turned_ref, sem_ops)
    keep.start()

    def update_pieces(columns, out):
        state = {}

        def store(q):
            rows = dot_nt(state.pop(("x", q)), state.pop(("w", q)))
            out[q * LANES : (q + 1) * LANES, :] = rows

        def select(q):
            state["x", q] = select_rows(q, state).astype(BF16)

        pieces = []
        for q in range(SEGMENT + 2):
            if q < SEGMENT:
                pieces.append(lambda q=q: fetch_rows(columns, q, table, state))
            if 1 <= q <= SEGMENT:
                pieces.extend(weight_pieces(staged, q - 1, state))
                pieces.append(lambda q=q: select(q - 1))
            if q >= 2:
                pieces.append(lambda q=q: store(q - 2))
        return pieces

    def scatter(index, update, first):
        rows = range(first, first + BANKS)
        where = [index[row // LANES, row % LANES] for row in rows]
        held = [banks[b][pl.ds(where[b], 1), :] for b in range(BANKS)]
        for b, row in enumerate(rows):
            banks[b][pl.ds(where[b], 1), :] = held[b] + update[row : row + 1, :]

    def both(segment, out, index, update):
        columns = pair_codes(targets, counts, segment).T
        first = OFFSETS - 1 - segment * SEGMENT
        stage_operators(turned, staged, [jnp.maximum(first - q, 0) for q in range(SEGMENT)])
        pieces = update_pieces(columns, out)
        batches = [lambda i=i: scatter(index, update, i) for i in range(0, ROWS, BANKS)]
        if WEAVE:
            weave(pieces, batches)
        else:
            weave(pieces, [])
            weave([lambda: None], batches)

    @pl.loop(0, STEPS)
    def _(step):
        fetch_index(partners, 2 * step - 1, index_e, sem_e).wait()
        fetch_index(partners, 2 * step, index_o, sem_o).start()
        both(2 * step, update_a, index_e, update_b)
        fetch_index(partners, 2 * step, index_o, sem_o).wait()
        fetch_index(partners, 2 * step + 1, index_e, sem_e).start()
        both(2 * step + 1, update_b, index_o, update_a)

    fetch_index(partners, 2 * STEPS - 1, index_e, sem_e).wait()
    for first in range(0, OFFSETS % SEGMENT * LANES, BANKS):
        scatter(index_e, update_b, first)

    left = left_half((32, LANES))

    def total(start, size):
        parts = [bank[pl.ds(start, size), :] for bank in banks]
        while len(parts) > 1:
            parts = [
                parts[i] + parts[i + 1] if i + 1 < len(parts) else parts[i]
                for i in range(0, len(parts), 2)
            ]
        return both_halves(parts[0])

    @pl.loop(0, CELLS // 256)
    def _(i):
        for j in range(4):
            start = pl.multiple_of(i * 256 + j * 64, 64)
            local_ref[pl.ds(start, 64), :] = total(start, 64)

    @pl.loop(0, 32)
    def _(i):
        for j in range(4):
            rows = total(pl.multiple_of(CELLS + i * 256 + j * 64, 64), 64)
            remote_ref[4 * i + j] = jnp.where(left, rows[:32], rows[32:])

    keep.wait()


def pair_scratch():
    return [
        pltpu.VMEM((COEF // 2 * OFFSETS, LANES), F32),
        pltpu.VMEM((COEF // 2 * SEGMENT, LANES), F32),
        pltpu.VMEM((PADDED, LANES), jnp.int32),
        pltpu.VMEM((PADDED, LANES), jnp.int32),
        pltpu.VMEM((ROWS, LANES), F32),
        pltpu.VMEM((ROWS, LANES), F32),
        pltpu.SMEM((SEGMENT, LANES), jnp.int32),
        pltpu.SMEM((SEGMENT, LANES), jnp.int32),
    ] + [pltpu.SemaphoreType.DMA] * 5


def partner_sums(counts, partners, targets, operators, multipoles):
    return pl.pallas_call(
        partner_kernel,
        name="partner_sums",
        out_shape=(
            jax.ShapeDtypeStruct((CELLS, LANES), F32),
            jax.ShapeDtypeStruct((128, 32, LANES), F32),
            jax.ShapeDtypeStruct((COEF // 2 * OFFSETS, LANES), F32),
        ),
        in_specs=[SMEM_SPEC, HBM_SPEC, HBM_SPEC, HBM_SPEC, VMEM_SPEC],
        out_specs=(VMEM_SPEC, VMEM_SPEC, HBM_SPEC),
        scratch_shapes=[
            pltpu.VMEM((COEF, COEF, OFFSETS), F32),
            pltpu.VMEM((HALF, 2 * LANES), BF16),
        ]
        + pair_scratch()
        + [pltpu.VMEM((TABLE, LANES), F32)] * BANKS,
        compiler_params=pltpu.CompilerParams(vmem_limit_bytes=VMEM_LIMIT),
        cost_estimate=pl.CostEstimate(
            flops=200_000_000_000, bytes_accessed=20_000_000, transcendentals=0
        ),
    )(counts, partners, targets, operators, multipoles)


def target_kernel(
    counts,
    partners_ref,
    targets_ref,
    turned_ref,
    multipoles_ref,
    fetched_ref,
    out_ref,
    table,
    total,
    *scratch,
):
    (turned, staged, partners, targets, rows_a, rows_b, index_e, index_o) = scratch[:8]
    sem_e, sem_o, sem_ops, sem_p, sem_t = scratch[8:]

    load = pltpu.make_async_copy(turned_ref, turned, sem_ops)
    load.start()
    load_pairs(partners_ref, targets_ref, partners, targets, sem_p, sem_t)
    fetch_index(partners, 0, index_e, sem_e).start()
    table[:CELLS, :] = cell_table(multipoles_ref[...])
    rows_b[...] = jnp.zeros_like(rows_b)
    total[...] = jnp.zeros_like(total)

    @pl.loop(0, 32)
    def _(i):
        for j in range(4):
            start = pl.multiple_of(CELLS + (4 * i + j) * 64, 64)
            table[pl.ds(start, 64), :] = unpack_rows(fetched_ref[4 * i + j])

    load.wait()

    def gather(index, rows, start, stop):
        for r in range(start, stop):
            rows[r : r + 1, :] = table[pl.ds(index[r // LANES, r % LANES], 1), :]

    def stage(segment):
        first = segment * SEGMENT
        ks = [jnp.clip(first + q, 0, OFFSETS - 1) for q in range(SEGMENT)]
        stage_operators(turned, staged, ks)
        return pair_codes(targets, counts, segment)

    def sum_pieces(codes, rows, count):
        state = {}
        low = codes & DEAD

        def product(q):
            x = rows[q * LANES : (q + 1) * LANES, :].astype(BF16)
            state["u", q] = dot_nt(state.pop(("w", q)), x)

        def add_halves(q):
            both = state.pop(("u", q))
            summed = both[:COEF] + both[COEF:]
            hi = summed.astype(BF16).astype(F32)
            state["v", q] = jnp.concatenate([hi, summed - hi], axis=0)

        def spread(q):
            upper = jnp.broadcast_to(codes[q : q + 1, :], (LANES, LANES)) > DEAD
            part = state.pop(("v", q))
            state["s", q] = jnp.concatenate(
                [jnp.where(upper, 0.0, part), jnp.where(upper, part, 0.0)], axis=0
            ).astype(BF16)

        def collect(p, start):
            picks = range(p * DEPTH, (p + 1) * DEPTH)
            spreads = jnp.concatenate([state["s", q] for q in picks], axis=1)
            total[start : start + MTILE, :] += dot_nt(hot_columns(low, picks, start, MTILE), spreads)

        pieces = []
        for q in range(count + 2):
            if q < count:
                pieces.extend(weight_pieces(staged, q, state))
                pieces.append(lambda q=q: product(q))
            if 1 <= q <= count:
                pieces.append(lambda q=q: add_halves(q - 1))
                pieces.append(lambda q=q: spread(q - 1))
            if q >= 2 and (q - 1) % DEPTH == 0:
                for start in range(0, HALF, MTILE):
                    pieces.append(lambda p=(q - 2) // DEPTH, start=start: collect(p, start))
        return pieces

    def both(segment, done, index, rows):
        codes = stage(segment)
        weave(
            sum_pieces(codes, done, SEGMENT),
            [lambda i=i: gather(index, rows, i, i + BATCH) for i in range(0, ROWS, BATCH)],
        )

    @pl.loop(0, STEPS)
    def _(step):
        fetch_index(partners, 2 * step, index_e, sem_e).wait()
        fetch_index(partners, 2 * step + 1, index_o, sem_o).start()
        both(2 * step - 1, rows_b, index_e, rows_a)
        fetch_index(partners, 2 * step + 1, index_o, sem_o).wait()
        fetch_index(partners, 2 * step + 2, index_e, sem_e).start()
        both(2 * step, rows_a, index_o, rows_b)

    fetch_index(partners, 2 * STEPS, index_e, sem_e).wait()
    weave(sum_pieces(stage(2 * STEPS - 1), rows_b, OFFSETS % SEGMENT), [])
    out_ref[...] = total[...]


def target_sums(counts, partners, targets, turned, multipoles, fetched):
    return pl.pallas_call(
        target_kernel,
        name="target_sums",
        out_shape=jax.ShapeDtypeStruct((HALF, 2 * LANES), F32),
        in_specs=[SMEM_SPEC, HBM_SPEC, HBM_SPEC, HBM_SPEC, VMEM_SPEC, VMEM_SPEC],
        out_specs=VMEM_SPEC,
        scratch_shapes=[
            pltpu.VMEM((TABLE, LANES), F32),
            pltpu.VMEM((HALF, 2 * LANES), F32),
        ]
        + pair_scratch(),
        compiler_params=pltpu.CompilerParams(vmem_limit_bytes=VMEM_LIMIT),
        cost_estimate=pl.CostEstimate(
            flops=200_000_000_000, bytes_accessed=20_000_000, transcendentals=0
        ),
    )(counts, partners, targets, turned, multipoles, fetched)


def finish_kernel(
    counts, cells_ref, returned_ref, parent_ref, partner_ref, target_ref, out_ref, total
):
    total[...] = target_ref[...]

    @pl.loop(0, 8)
    def _(segment):
        codes = slot_codes(cells_ref, counts, segment)
        columns = codes.T
        spreads = []
        for q in range(SEGMENT):
            packed = returned_ref[pl.ds(segment * 2 * SEGMENT + 2 * q, 2)]
            rows = unpack_rows(packed).reshape(LANES, LANES)
            upper = jnp.broadcast_to(columns[:, q : q + 1], (LANES, LANES)) > DEAD
            spreads.append(
                jnp.concatenate(
                    [jnp.where(upper, 0.0, rows), jnp.where(upper, rows, 0.0)], axis=1
                ).astype(BF16)
            )
        hot = hot_columns(codes & DEAD, range(SEGMENT), 0, HALF)
        total[...] += dot_nn(hot, jnp.concatenate(spreads, axis=0))

    for half in range(2):
        summed = both_halves(total[:, half * LANES : (half + 1) * LANES])
        summed = summed + partner_ref[half * HALF : (half + 1) * HALF]
        columns = slice(half * HALF, (half + 1) * HALF)
        out_ref[:, columns] = parent_ref[:, columns] + summed.T[:COEF]


def finish(counts, cells, returned, parent_locals, partner_part, target_part):
    return pl.pallas_call(
        finish_kernel,
        name="finish",
        out_shape=jax.ShapeDtypeStruct((COEF, CELLS), F32),
        in_specs=[SMEM_SPEC] + [VMEM_SPEC] * 5,
        out_specs=VMEM_SPEC,
        scratch_shapes=[pltpu.VMEM((HALF, 2 * LANES), F32)],
        compiler_params=pltpu.CompilerParams(vmem_limit_bytes=VMEM_LIMIT),
    )(counts, cells, returned, parent_locals, partner_part, target_part)


def shards(
    multipoles,
    parent_locals,
    operators,
    pair_target,
    pair_partner,
    pair_count,
    send_cells,
    send_count,
):
    axes = ("row", "col")
    cells = send_cells.reshape(16, 4, LANES)
    ops = operators.transpose(1, 2, 0)
    outgoing = send_rows(send_count, cells, multipoles)
    fetched = exchange(outgoing, axes)
    partner_part, returning, turned = partner_sums(
        pair_count, pair_partner, pair_target, ops, multipoles
    )
    returned = exchange(returning, axes)
    target_part = target_sums(pair_count, pair_partner, pair_target, turned, multipoles, fetched)
    return finish(send_count, cells, returned, parent_locals, partner_part, target_part)


def exchange(blocks, axes):
    return lax.all_to_all(blocks, axes, split_axis=0, concat_axis=0, tiled=True)


def solution(mesh):
    in_specs = (
        P(None, ("row", "col")),
        P(None, ("row", "col")),
        P(),
        P(None, ("row", "col")),
        P(None, ("row", "col")),
        P(("row", "col"), None),
        P(("row", "col"), None),
        P(("row", "col"), None),
    )
    out_specs = P(None, ("row", "col"))
    return jax.shard_map(shards, mesh=mesh, in_specs=in_specs, out_specs=out_specs, check_vma=False)
```

time: 1050 us -> 185 us (0.18)
  other arithmetic: 556 us -> 0 us
  local copies, waits for them, and re-layouts: 331 us -> 0 us
  Pallas kernels: 0 us -> 162 us
  matrix products: 93.1 us -> 0 us
  waiting for transfers between devices: 34.2 us -> 0.01 us
  loops' own time: 16.2 us -> 0 us
    scatter-add x5 -> x0, other arithmetic: 458 us -> none  [the longest x4 414 us: one_group(): summed = summed.at[landing].add(update_rows)]
    gather x7 -> x0, local copies, waits for them, and re-layouts: 237 us -> none  [the longest x4 161 us: one_group(): jnp.take(table_rows, both_ids, axis=0)]
    pallas_call x0 -> x4, Pallas kernels: none -> 162 us  [the longest x1 84.8 us: partner_sums(): pl.pallas_call(partner_kernel, name='partner_sums', out_shape=(jax.ShapeD...]
    dot_general x8 -> x0, matrix products: 93.1 us -> none  [the longest x4 46.6 us: one_group(): jnp.einsum('kij,kpj->kpi', forward, picked[0], precision=lax.Precision.HI...]
    select_n x16 -> x0, other arithmetic: 56.9 us -> none  [the longest x8 48 us: one_group(): jnp.take(table_rows, both_ids, axis=0)]
    all_to_all x2, waiting for transfers between devices: 34.2 us -> 0.01 us  [exchange(): return lax.all_to_all(blocks, axes, split_axis=0, concat_axis=0, tiled=True)]
    reshape x5 -> x0, local copies, waits for them, and re-layouts: 33.6 us -> none  [the longest x4 33.5 us: one_group(): jnp.concatenate([to_target, to_partner], axis=0).reshape(-1, components)]
    unnamed x25 -> x0, local copies, waits for them, and re-layouts: 21 us -> none
  transfers between devices with their start and end apart: 2 -> 2, of which waited for: 2 -> 0; matrix products, arithmetic and copies ran while one was open for 2% -> 0% of each run, Pallas kernels for 0% -> 79%
where the time goes in v2:
time: 185 us; the launch traced here: 184 us
  Pallas kernels  162 us (88%)
  starting transfers between devices  22.2 us (12%)
    pallas_call x1, Pallas kernels, partner_sums(): pl.pallas_call(partner_kernel, name='partner_sums', out_shape=(jax.ShapeD...  84.8 us
    pallas_call x1, Pallas kernels, target_sums(): pl.pallas_call(target_kernel, name='target_sums', out_shape=jax.ShapeDtyp...  60.4 us
    all_to_all x2, starting transfers between devices, exchange(): return lax.all_to_all(blocks, axes, split_axis=0, concat_axis=0, tiled=True)  22.2 us
    pallas_call x1, Pallas kernels, finish(): pl.pallas_call(finish_kernel, name='finish', out_shape=jax.ShapeDtypeStru...  8.98 us
    pallas_call x1, Pallas kernels, send_rows(): pl.pallas_call(send_kernel, name='send_rows', out_shape=jax.ShapeDtypeStr...  7.88 us
  transfers between devices with their start and end apart: 2, of which 0 were waited for; matrix products, arithmetic and copies ran while one was open for 0% of the time, Pallas kernels for 79%

profile of v2, /device:TPU:1, one launch (start us, length us, event | category | flops | bytes accessed | tf_op | source)
XLA Modules:
  0.0 184.2 jit_solution(14664336801059654492)
XLA Ops:
  0.0 7.9 %send_rows.1 = f32[128,32,128]{2,1,0:T(8,128)} custom-call(s32[1,128]{1,0:T(1,128)} %counts.7, s32[16,4,128]{2,1,0:T(4,128)} %bitcast.2, f32[64,1024]{1,0:T(8,128)} %multipoles_ref.5), custom_call_target="tpu_custom_call" | custom-call | tf_op jit(solution)/shard_map/send_rows/pallas_call | solution.py:198
  7.9 11.9 %all-to-all-start.1 = ((f32[128,32,128]{2,1,0:T(8,128)}), f32[128,32,128]{2,1,0:T(8,128)}, u32[]{:S(2)}, u32[]{:S(2)}) async-start(f32[128,32,128]{2,1,0:T(8,128)} %send_rows.1), calls=%async_computation.1 | async-start | bytes 4194304 | tf_op jit(solution)/shard_map/all_to_all | solution.py:562
  19.8 84.8 %partner_sums.1 = (f32[1024,128]{1,0:T(8,128)}, f32[128,32,128]{2,1,0:T(8,128)}, f32[10112,128]{1,0:T(8,128)}) custom-call(s32[1,316]{1,0:T(1,128)} %counts.6, s32[316,128]{1,0:T(8,128)} %partners_ref.3, s32[316,128]{1,0:T(8,128)} %targets_ref.3, f32[64,64,316]{2,1,0:T(8,128)} %bitcast.4, f32[64,1024]{1,0:T(8,128)} %multipoles_ref.5), custom_call_target="tpu_custom_call" | custom-call | flops 199999995904 | bytes 20000000 | tf_op jit(solution)/shard_map/partner_sums/pallas_call | solution.py:354
  104.6 0.0 all-to-all-done.1.fetched_ref
  104.6 10.2 %all-to-all-start = ((f32[128,32,128]{2,1,0:T(8,128)}), f32[128,32,128]{2,1,0:T(8,128)}, u32[]{:S(2)}, u32[]{:S(2)}) async-start(f32[128,32,128]{2,1,0:T(8,128)} %get-tuple-element.8), calls=%async_computation | async-start | bytes 4194304 | tf_op jit(solution)/shard_map/all_to_all | solution.py:562
  114.9 60.4 %target_sums.1.target_ref = f32[512,256]{1,0:T(8,128)} custom-call(s32[1,316]{1,0:T(1,128)} %counts.6, s32[316,128]{1,0:T(8,128)} %partners_ref.3, s32[316,128]{1,0:T(8,128)} %targets_ref.3, f32[10112,128]{1,0:T(8,128)} %get-tuple-element.10.turned_ref, f32[64,1024]{1,0:T(8,128)} %multipoles_ref.5, f32[128,32,128]{2,1,0:T(8,128)} %all-to-all-done.1.fetched_ref), custom_call_target="tpu_custom_call" | custom-call | flops 199999995904 | bytes 20000000 | tf_op jit(solution)/shard_map/target_sums/pallas_call | solution.py:479
  175.2 0.0 all-to-all-done.returned_ref
  175.2 9.0 %finish.1 = f32[64,1024]{1,0:T(8,128)} custom-call(s32[1,128]{1,0:T(1,128)} %counts.7, s32[16,4,128]{2,1,0:T(4,128)} %bitcast.3, f32[128,32,128]{2,1,0:T(8,128)} %all-to-all-done.returned_ref, f32[64,1024]{1,0:T(8,128)} %parent_ref.1, f32[1024,128]{1,0:T(8,128)} %get-tuple-element.9.partner_ref, f32[512,256]{1,0:T(8,128)} %target_sums.1.target_ref), custom_call_target="tpu_custom_call" | custom-call | tf_op jit(solution)/shard_map/finish/pallas_call | solution.py:527
Async XLA Ops:
  7.9 96.7 %all-to-all-start.1 = ((f32[128,32,128]{2,1,0:T(8,128)}), f32[128,32,128]{2,1,0:T(8,128)}, u32[]{:S(2)}, u32[]{:S(2)}) async-start(f32[128,32,128]{2,1,0:T(8,128)} %send_rows.1), calls=%async_computation.1 | async-start | bytes 4194304 | tf_op jit(solution)/shard_map/all_to_all | solution.py:562
  104.6 70.6 %all-to-all-start = ((f32[128,32,128]{2,1,0:T(8,128)}), f32[128,32,128]{2,1,0:T(8,128)}, u32[]{:S(2)}, u32[]{:S(2)}) async-start(f32[128,32,128]{2,1,0:T(8,128)} %get-tuple-element.8), calls=%async_computation | async-start | bytes 4194304 | tf_op jit(solution)/shard_map/all_to_all | solution.py:562

commit v3 on v2

--- a/solution.py
+++ b/solution.py
@@ -20,7 +20,11 @@
 STEPS = 20
 PADDED = 320
 DEAD = 0xFFFF
-BANKS = 8
+BANKS = 4
+FDEPTH = 4
+FSEGMENTS = 4
+TURN = 8
+PITCH = 33
 BATCH = 8
 DEPTH = 4
 WEAVE = False
@@ -45,20 +49,21 @@
 
 
 def turn_operators(ops_ref, turned):
-    @pl.loop(0, COEF // 2)
-    def _(p):
-        for start in range(0, OFFSETS, LANES):
-            size = min(LANES, OFFSETS - start)
-            pair = jnp.concatenate(
-                [ops_ref[p, :, start : start + size], ops_ref[p + 32, :, start : start + size]], axis=0
-            )
-            turned[pl.ds(start * (COEF // 2) + p, size, stride=COEF // 2), :] = pair.T
+    @pl.loop(0, COEF // 2 // TURN)
+    def _(i):
+        for t in range(TURN):
+            p = i * TURN + t
+            for start in range(0, OFFSETS, LANES):
+                size = min(LANES, OFFSETS - start)
+                lanes = slice(start, start + size)
+                pair = jnp.concatenate([ops_ref[p, :, lanes], ops_ref[p + 32, :, lanes]], axis=0)
+                turned[pl.ds(start * PITCH + p, size, stride=PITCH), :] = pair.T
 
 
 def stage_operators(turned, staged, ks):
     size = COEF // 2
     for q, k in enumerate(ks):
-        staged[q * size : (q + 1) * size, :] = turned[pl.ds(pl.multiple_of(k * size, size), size), :]
+        staged[q * size : (q + 1) * size, :] = turned[pl.ds(k * PITCH, size), :]
 
 
 def weave(pieces, batches):
@@ -99,8 +104,9 @@
 
 
 def folded_table(multipoles):
-    table = cell_table(multipoles).astype(BF16)
-    return jnp.concatenate([table[:HALF], table[HALF:]], axis=1)
+    hi, lo = multipoles.astype(BF16), multipoles - multipoles.astype(BF16).astype(F32)
+    both = jnp.concatenate([hi, lo.astype(BF16)], axis=0)
+    return jnp.concatenate([both[:, :HALF], both[:, HALF:]], axis=0)
 
 
 def pair_codes(targets, counts, segment):
@@ -130,29 +136,51 @@
     return jnp.where(live, (cells & (HALF - 1)) + ((cells >> 9) << 16), DEAD)
 
 
-def spread_column(columns, q):
-    code = jnp.broadcast_to(columns[:, q : q + 1], (LANES, LANES))
-    lane = lax.broadcasted_iota(jnp.int32, (LANES, LANES), 1)
-    low = code & DEAD
-    hot = [(low == lane + start).astype(F32).astype(BF16) for start in range(0, HALF, LANES)]
-    return jnp.concatenate(hot, axis=1), code > DEAD
-
-
-def fetch_rows(columns, q, table, state):
-    hot, upper = spread_column(columns, q)
-    state["both", q] = dot_nn(hot, table[...])
-    state["upper", q] = upper
-
-
-def select_rows(q, state):
+def fetch_columns(codes, picks, table, state):
+    both = dot_nn(table[...], hot_columns(codes & DEAD, picks, 0, HALF))
+    for i, q in enumerate(picks):
+        state["both", q] = both[:, i * LANES : (i + 1) * LANES]
+
+
+def select_columns(codes, q, state):
     part = state.pop(("both", q))
-    return jnp.where(state.pop(("upper", q)), part[:, LANES:], part[:, :LANES])
+    upper = jnp.broadcast_to(codes[q : q + 1, :], (LANES, LANES)) > DEAD
+    return jnp.where(upper, part[LANES:], part[:LANES])
 
 
 def hot_columns(low, picks, start, size):
     cell = lax.broadcasted_iota(jnp.int32, (size, LANES), 0) + start
     hot = [(low[q : q + 1, :] == cell).astype(F32).astype(BF16) for q in picks]
     return jnp.concatenate(hot, axis=1)
+
+
+def pack_columns(columns):
+    left = left_half((32, LANES))
+    top, bottom = columns[:32], columns[32:]
+    return (
+        jnp.where(left, top, pltpu.roll(bottom, COEF, 1)),
+        jnp.where(left, pltpu.roll(top, COEF, 1), bottom),
+    )
+
+
+def unpack_columns(first, second):
+    left = left_half((32, LANES))
+    return [
+        jnp.where(left, first, pltpu.roll(second, COEF, 1)),
+        jnp.where(left, pltpu.roll(first, COEF, 1), second),
+    ]
+
+
+def hi_lo(x):
+    hi = x.astype(BF16).astype(F32)
+    return jnp.concatenate([hi, x - hi], axis=0)
+
+
+def spread_codes(codes, q, part):
+    upper = jnp.broadcast_to(codes[q : q + 1, :], (LANES, LANES)) > DEAD
+    return jnp.concatenate(
+        [jnp.where(upper, 0.0, part), jnp.where(upper, part, 0.0)], axis=0
+    ).astype(BF16)
 
 
 def unpack_rows(packed):
@@ -171,21 +199,24 @@
 
     @pl.loop(0, 8)
     def _(segment):
-        columns = slot_codes(cells_ref, counts, segment).T
+        codes = slot_codes(cells_ref, counts, segment)
         state = {}
 
         def store(q):
-            rows = both_halves(select_rows(q, state))
+            x = select_columns(codes, q, state)
+            x = x[:COEF] + x[COEF:]
+            rows = jnp.concatenate([x, x], axis=0).T
             for b in range(2):
                 base = b * 64
                 out_ref[segment * 2 * SEGMENT + 2 * q + b] = jnp.where(
                     left, rows[base : base + 32], rows[base + 32 : base + 64]
                 )
 
-        for q in range(SEGMENT + 1):
+        for q in range(0, SEGMENT + 2, 2):
             if q < SEGMENT:
-                fetch_rows(columns, q, table, state)
-            if q >= 1:
+                fetch_columns(codes, range(q, q + 2), table, state)
+            if q >= 2:
+                store(q - 2)
                 store(q - 1)
 
 
@@ -201,7 +232,7 @@
         out_shape=jax.ShapeDtypeStruct((128, 32, LANES), F32),
         in_specs=[SMEM_SPEC, VMEM_SPEC, VMEM_SPEC],
         out_specs=VMEM_SPEC,
-        scratch_shapes=[pltpu.VMEM((HALF, 2 * LANES), BF16)],
+        scratch_shapes=[pltpu.VMEM((2 * LANES, HALF), BF16)],
         compiler_params=pltpu.CompilerParams(vmem_limit_bytes=VMEM_LIMIT),
     )(counts, cells, multipoles)
 
@@ -218,6 +249,10 @@
     ]
     for copy in copies:
         copy.start()
+    return copies
+
+
+def finish_pairs(copies, partners, targets):
     for copy in copies:
         copy.wait()
     for pairs in (partners, targets):
@@ -243,9 +278,9 @@
 
     load = pltpu.make_async_copy(ops_ref, native, sem_ops)
     load.start()
-    load_pairs(partners_ref, targets_ref, partners, targets, sem_p, sem_t)
-    fetch_index(partners, 0, index_e, sem_e).start()
+    pairs = load_pairs(partners_ref, targets_ref, partners, targets, sem_p, sem_t)
     table[...] = folded_table(multipoles_ref[...])
+    update_a[...] = jnp.zeros_like(update_a)
     update_b[...] = jnp.zeros_like(update_b)
 
     @pl.loop(0, TABLE // 128)
@@ -253,45 +288,60 @@
         for bank in banks:
             bank[pl.ds(pl.multiple_of(i * 128, 128), 128), :] = jnp.zeros((128, LANES), F32)
 
+    finish_pairs(pairs, partners, targets)
+    fetch_index(partners, 0, index_e, sem_e).start()
     load.wait()
     turn_operators(native, turned)
     keep = pltpu.make_async_copy(turned, turned_ref, sem_ops)
     keep.start()
 
-    def update_pieces(columns, out):
+    def update_pieces(codes, out):
         state = {}
 
+        def product(q):
+            both = dot_nn(state.pop(("w", q)), state.pop(("x", q)))
+            state["u", q] = both[:COEF] + both[COEF:]
+
         def store(q):
-            rows = dot_nt(state.pop(("x", q)), state.pop(("w", q)))
-            out[q * LANES : (q + 1) * LANES, :] = rows
+            pair = jnp.concatenate([state.pop(("u", q)), state.pop(("u", q + 1))], axis=0)
+            out[q // 2 * LANES : (q // 2 + 1) * LANES, :] = pair.T
 
         def select(q):
-            state["x", q] = select_rows(q, state).astype(BF16)
+            state["x", q] = select_columns(codes, q, state).astype(BF16)
 
         pieces = []
-        for q in range(SEGMENT + 2):
+        for q in range(0, SEGMENT + 4, 2):
             if q < SEGMENT:
-                pieces.append(lambda q=q: fetch_rows(columns, q, table, state))
-            if 1 <= q <= SEGMENT:
-                pieces.extend(weight_pieces(staged, q - 1, state))
-                pieces.append(lambda q=q: select(q - 1))
-            if q >= 2:
-                pieces.append(lambda q=q: store(q - 2))
+                pieces.append(lambda q=q: fetch_columns(codes, range(q, q + 2), table, state))
+            for r in (q - 2, q - 1):
+                if 0 <= r < SEGMENT:
+                    pieces.extend(weight_pieces(staged, r, state))
+                    pieces.append(lambda r=r: select(r))
+            for r in (q - 4, q - 3):
+                if r >= 0:
+                    pieces.append(lambda r=r: product(r))
+            if q >= 4:
+                pieces.append(lambda q=q: store(q - 4))
         return pieces
 
     def scatter(index, update, first):
         rows = range(first, first + BANKS)
-        where = [index[row // LANES, row % LANES] for row in rows]
-        held = [banks[b][pl.ds(where[b], 1), :] for b in range(BANKS)]
-        for b, row in enumerate(rows):
-            banks[b][pl.ds(where[b], 1), :] = held[b] + update[row : row + 1, :]
+        left = left_half((1, LANES))
+        parts = []
+        for side, mask in ((0, left), (1, ~left)):
+            for bank, row in zip(banks, rows):
+                where = index[row // LANES * 2 + side, row % LANES]
+                view = bank.at[pl.ds(where, 1), :]
+                parts.append((view, mask, view[...], row))
+        for view, mask, held, row in parts:
+            pltpu.store(view, held + update[row : row + 1, :], mask=mask)
 
     def both(segment, out, index, update):
-        columns = pair_codes(targets, counts, segment).T
+        codes = pair_codes(targets, counts, segment)
         first = OFFSETS - 1 - segment * SEGMENT
         stage_operators(turned, staged, [jnp.maximum(first - q, 0) for q in range(SEGMENT)])
-        pieces = update_pieces(columns, out)
-        batches = [lambda i=i: scatter(index, update, i) for i in range(0, ROWS, BANKS)]
+        pieces = update_pieces(codes, out)
+        batches = [lambda i=i: scatter(index, update, i) for i in range(0, ROWS // 2, BANKS)]
         if WEAVE:
             weave(pieces, batches)
         else:
@@ -308,10 +358,8 @@
         both(2 * step + 1, update_b, index_o, update_a)
 
     fetch_index(partners, 2 * STEPS - 1, index_e, sem_e).wait()
-    for first in range(0, OFFSETS % SEGMENT * LANES, BANKS):
+    for first in range(0, OFFSETS % SEGMENT * LANES // 2, BANKS):
         scatter(index_e, update_b, first)
-
-    left = left_half((32, LANES))
 
     def total(start, size):
         parts = [bank[pl.ds(start, size), :] for bank in banks]
@@ -320,26 +368,27 @@
                 parts[i] + parts[i + 1] if i + 1 < len(parts) else parts[i]
                 for i in range(0, len(parts), 2)
             ]
-        return both_halves(parts[0])
+        return parts[0]
 
     @pl.loop(0, CELLS // 256)
     def _(i):
-        for j in range(4):
-            start = pl.multiple_of(i * 256 + j * 64, 64)
-            local_ref[pl.ds(start, 64), :] = total(start, 64)
-
-    @pl.loop(0, 32)
+        start = pl.multiple_of(i * 256, 256)
+        local_ref[pl.ds(start, 256), :] = both_halves(total(start, 256))
+
+    @pl.loop(0, 16)
     def _(i):
         for j in range(4):
-            rows = total(pl.multiple_of(CELLS + i * 256 + j * 64, 64), 64)
-            remote_ref[4 * i + j] = jnp.where(left, rows[:32], rows[32:])
+            both = total(pl.multiple_of(CELLS + i * 512 + j * LANES, LANES), LANES).T
+            first, second = pack_columns(both[:COEF] + both[COEF:])
+            remote_ref[8 * i + 2 * j] = first
+            remote_ref[8 * i + 2 * j + 1] = second
 
     keep.wait()
 
 
 def pair_scratch():
     return [
-        pltpu.VMEM((COEF // 2 * OFFSETS, LANES), F32),
+        pltpu.VMEM((PITCH * OFFSETS, LANES), F32),
         pltpu.VMEM((COEF // 2 * SEGMENT, LANES), F32),
         pltpu.VMEM((PADDED, LANES), jnp.int32),
         pltpu.VMEM((PADDED, LANES), jnp.int32),
@@ -357,13 +406,13 @@
         out_shape=(
             jax.ShapeDtypeStruct((CELLS, LANES), F32),
             jax.ShapeDtypeStruct((128, 32, LANES), F32),
-            jax.ShapeDtypeStruct((COEF // 2 * OFFSETS, LANES), F32),
+            jax.ShapeDtypeStruct((PITCH * OFFSETS, LANES), F32),
         ),
         in_specs=[SMEM_SPEC, HBM_SPEC, HBM_SPEC, HBM_SPEC, VMEM_SPEC],
         out_specs=(VMEM_SPEC, VMEM_SPEC, HBM_SPEC),
         scratch_shapes=[
             pltpu.VMEM((COEF, COEF, OFFSETS), F32),
-            pltpu.VMEM((HALF, 2 * LANES), BF16),
+            pltpu.VMEM((2 * LANES, HALF), BF16),
         ]
         + pair_scratch()
         + [pltpu.VMEM((TABLE, LANES), F32)] * BANKS,
@@ -391,8 +440,7 @@
 
     load = pltpu.make_async_copy(turned_ref, turned, sem_ops)
     load.start()
-    load_pairs(partners_ref, targets_ref, partners, targets, sem_p, sem_t)
-    fetch_index(partners, 0, index_e, sem_e).start()
+    pairs = load_pairs(partners_ref, targets_ref, partners, targets, sem_p, sem_t)
     table[:CELLS, :] = cell_table(multipoles_ref[...])
     rows_b[...] = jnp.zeros_like(rows_b)
     total[...] = jnp.zeros_like(total)
@@ -403,6 +451,8 @@
             start = pl.multiple_of(CELLS + (4 * i + j) * 64, 64)
             table[pl.ds(start, 64), :] = unpack_rows(fetched_ref[4 * i + j])
 
+    finish_pairs(pairs, partners, targets)
+    fetch_index(partners, 0, index_e, sem_e).start()
     load.wait()
 
     def gather(index, rows, start, stop):
@@ -425,16 +475,10 @@
 
         def add_halves(q):
             both = state.pop(("u", q))
-            summed = both[:COEF] + both[COEF:]
-            hi = summed.astype(BF16).astype(F32)
-            state["v", q] = jnp.concatenate([hi, summed - hi], axis=0)
+            state["v", q] = hi_lo(both[:COEF] + both[COEF:])
 
         def spread(q):
-            upper = jnp.broadcast_to(codes[q : q + 1, :], (LANES, LANES)) > DEAD
-            part = state.pop(("v", q))
-            state["s", q] = jnp.concatenate(
-                [jnp.where(upper, 0.0, part), jnp.where(upper, part, 0.0)], axis=0
-            ).astype(BF16)
+            state["s", q] = spread_codes(codes, q, state.pop(("v", q)))
 
         def collect(p, start):
             picks = range(p * DEPTH, (p + 1) * DEPTH)
@@ -499,22 +543,30 @@
 ):
     total[...] = target_ref[...]
 
-    @pl.loop(0, 8)
-    def _(segment):
-        codes = slot_codes(cells_ref, counts, segment)
-        columns = codes.T
+    def prepare(codes, segment, picks):
         spreads = []
-        for q in range(SEGMENT):
-            packed = returned_ref[pl.ds(segment * 2 * SEGMENT + 2 * q, 2)]
-            rows = unpack_rows(packed).reshape(LANES, LANES)
-            upper = jnp.broadcast_to(columns[:, q : q + 1], (LANES, LANES)) > DEAD
-            spreads.append(
-                jnp.concatenate(
-                    [jnp.where(upper, 0.0, rows), jnp.where(upper, rows, 0.0)], axis=1
-                ).astype(BF16)
-            )
-        hot = hot_columns(codes & DEAD, range(SEGMENT), 0, HALF)
-        total[...] += dot_nn(hot, jnp.concatenate(spreads, axis=0))
+        for q in picks:
+            block = segment * 2 * SEGMENT + 2 * q
+            columns = unpack_columns(returned_ref[block], returned_ref[block + 1])
+            spreads.append(spread_codes(codes, q, hi_lo(jnp.concatenate(columns, axis=0))))
+        return jnp.concatenate(spreads, axis=1)
+
+    @pl.loop(0, 8 // FSEGMENTS)
+    def _(trip):
+        segments = [trip * FSEGMENTS + i for i in range(FSEGMENTS)]
+        codes = [slot_codes(cells_ref, counts, segment) for segment in segments]
+        chunks = [
+            (i, range(p, p + FDEPTH)) for i in range(FSEGMENTS) for p in range(0, SEGMENT, FDEPTH)
+        ]
+        ready = prepare(codes[0], segments[0], chunks[0][1])
+        for n, (i, picks) in enumerate(chunks):
+            spreads = ready
+            if n + 1 < len(chunks):
+                j, ahead = chunks[n + 1]
+                ready = prepare(codes[j], segments[j], ahead)
+            for start in range(0, HALF, MTILE):
+                hot = hot_columns(codes[i] & DEAD, picks, start, MTILE)
+                total[start : start + MTILE, :] += dot_nt(hot, spreads)
 
     for half in range(2):
         summed = both_halves(total[:, half * LANES : (half + 1) * LANES])

time: 185 us -> 165 us (0.89)
  Pallas kernels: 162 us -> 143 us
    pallas_call x1, Pallas kernels: 84.8 us -> 71.5 us  [partner_sums(): pl.pallas_call(partner_kernel, name='partner_sums', out_shape=(jax.ShapeD...]
    pallas_call x1, Pallas kernels: 8.98 us -> 5.74 us  [finish(): pl.pallas_call(finish_kernel, name='finish', out_shape=jax.ShapeDtypeStru...]
    pallas_call x1, Pallas kernels: 60.4 us -> 58.4 us  [target_sums(): pl.pallas_call(target_kernel, name='target_sums', out_shape=jax.ShapeDtyp...]
where the time goes in v3:
time: 165 us
  Pallas kernels  143 us (87%)
  starting transfers between devices  22.2 us (13%)
    pallas_call x1, Pallas kernels, partner_sums(): pl.pallas_call(partner_kernel, name='partner_sums', out_shape=(jax.ShapeD...  71.5 us
    pallas_call x1, Pallas kernels, target_sums(): pl.pallas_call(target_kernel, name='target_sums', out_shape=jax.ShapeDtyp...  58.4 us
    all_to_all x2, starting transfers between devices, exchange(): return lax.all_to_all(blocks, axes, split_axis=0, concat_axis=0, tiled=True)  22.2 us
    pallas_call x1, Pallas kernels, send_rows(): pl.pallas_call(send_kernel, name='send_rows', out_shape=jax.ShapeDtypeStr...  6.97 us
    pallas_call x1, Pallas kernels, finish(): pl.pallas_call(finish_kernel, name='finish', out_shape=jax.ShapeDtypeStru...  5.74 us
  transfers between devices with their start and end apart: 2, of which 0 were waited for; matrix products, arithmetic and copies ran while one was open for 0% of the time, Pallas kernels for 79%

profile of v3, /device:TPU:1, one launch (start us, length us, event | category | flops | bytes accessed | tf_op | source)
XLA Modules:
  0.0 164.9 jit_solution(13600337275629176880)
XLA Ops:
  0.0 7.0 %send_rows.1 = f32[128,32,128]{2,1,0:T(8,128)} custom-call(s32[1,128]{1,0:T(1,128)} %counts.7, s32[16,4,128]{2,1,0:T(4,128)} %bitcast.2, f32[64,1024]{1,0:T(8,128)} %multipoles_ref.5), custom_call_target="tpu_custom_call" | custom-call | tf_op jit(solution)/shard_map/send_rows/pallas_call | solution.py:229
  7.0 11.9 %all-to-all-start.1 = ((f32[128,32,128]{2,1,0:T(8,128)}), f32[128,32,128]{2,1,0:T(8,128)}, u32[]{:S(2)}, u32[]{:S(2)}) async-start(f32[128,32,128]{2,1,0:T(8,128)} %send_rows.1), calls=%async_computation.1 | async-start | bytes 4194304 | tf_op jit(solution)/shard_map/all_to_all | solution.py:614
  18.9 71.5 %partner_sums.1 = (f32[1024,128]{1,0:T(8,128)}, f32[128,32,128]{2,1,0:T(8,128)}, f32[10428,128]{1,0:T(8,128)}) custom-call(s32[1,316]{1,0:T(1,128)} %counts.6, s32[316,128]{1,0:T(8,128)} %partners_ref.3, s32[316,128]{1,0:T(8,128)} %targets_ref.3, f32[64,64,316]{2,1,0:T(8,128)} %bitcast.4, f32[64,1024]{1,0:T(8,128)} %multipoles_ref.5), custom_call_target="tpu_custom_call" | custom-call | flops 199999995904 | bytes 20000000 | tf_op jit(solution)/shard_map/partner_sums/pallas_call | solution.py:403
  90.5 0.0 all-to-all-done.1.fetched_ref
  90.5 10.2 %all-to-all-start = ((f32[128,32,128]{2,1,0:T(8,128)}), f32[128,32,128]{2,1,0:T(8,128)}, u32[]{:S(2)}, u32[]{:S(2)}) async-start(f32[128,32,128]{2,1,0:T(8,128)} %get-tuple-element.8), calls=%async_computation | async-start | bytes 4194304 | tf_op jit(solution)/shard_map/all_to_all | solution.py:614
  100.7 58.4 %target_sums.1.target_ref = f32[512,256]{1,0:T(8,128)} custom-call(s32[1,316]{1,0:T(1,128)} %counts.6, s32[316,128]{1,0:T(8,128)} %partners_ref.3, s32[316,128]{1,0:T(8,128)} %targets_ref.3, f32[10428,128]{1,0:T(8,128)} %get-tuple-element.10.turned_ref, f32[64,1024]{1,0:T(8,128)} %multipoles_ref.5, f32[128,32,128]{2,1,0:T(8,128)} %all-to-all-done.1.fetched_ref), custom_call_target="tpu_custom_call" | custom-call | flops 199999995904 | bytes 20000000 | tf_op jit(solution)/shard_map/target_sums/pallas_call | solution.py:523
  159.2 0.0 all-to-all-done.returned_ref
  159.2 5.7 %finish.1 = f32[64,1024]{1,0:T(8,128)} custom-call(s32[1,128]{1,0:T(1,128)} %counts.7, s32[16,4,128]{2,1,0:T(4,128)} %bitcast.3, f32[128,32,128]{2,1,0:T(8,128)} %all-to-all-done.returned_ref, f32[64,1024]{1,0:T(8,128)} %parent_ref.1, f32[1024,128]{1,0:T(8,128)} %get-tuple-element.9.partner_ref, f32[512,256]{1,0:T(8,128)} %target_sums.1.target_ref), custom_call_target="tpu_custom_call" | custom-call | tf_op jit(solution)/shard_map/finish/pallas_call | solution.py:579
Async XLA Ops:
  7.0 83.5 %all-to-all-start.1 = ((f32[128,32,128]{2,1,0:T(8,128)}), f32[128,32,128]{2,1,0:T(8,128)}, u32[]{:S(2)}, u32[]{:S(2)}) async-start(f32[128,32,128]{2,1,0:T(8,128)} %send_rows.1), calls=%async_computation.1 | async-start | bytes 4194304 | tf_op jit(solution)/shard_map/all_to_all | solution.py:614
  90.5 68.7 %all-to-all-start = ((f32[128,32,128]{2,1,0:T(8,128)}), f32[128,32,128]{2,1,0:T(8,128)}, u32[]{:S(2)}, u32[]{:S(2)}) async-start(f32[128,32,128]{2,1,0:T(8,128)} %get-tuple-element.8), calls=%async_computation | async-start | bytes 4194304 | tf_op jit(solution)/shard_map/all_to_all | solution.py:614

commit v4 on v3

--- a/solution.py
+++ b/solution.py
@@ -17,7 +17,9 @@
 OFFSETS = 316
 SEGMENT = 8
 ROWS = SEGMENT * LANES
-STEPS = 20
+SEGMENTS = 40
+PARTNER_SPAN = 4
+TARGET_SPAN = 2
 PADDED = 320
 DEAD = 0xFFFF
 BANKS = 4
@@ -26,7 +28,7 @@
 TURN = 8
 PITCH = 33
 BATCH = 8
-DEPTH = 4
+DEPTH = 2
 WEAVE = False
 MTILE = 256
 VMEM_LIMIT = 60 * 1024 * 1024
@@ -197,27 +199,35 @@
     table[...] = folded_table(multipoles_ref[...])
     left = left_half((32, LANES))
 
-    @pl.loop(0, 8)
-    def _(segment):
-        codes = slot_codes(cells_ref, counts, segment)
-        state = {}
-
-        def store(q):
-            x = select_columns(codes, q, state)
-            x = x[:COEF] + x[COEF:]
-            rows = jnp.concatenate([x, x], axis=0).T
-            for b in range(2):
-                base = b * 64
-                out_ref[segment * 2 * SEGMENT + 2 * q + b] = jnp.where(
-                    left, rows[base : base + 32], rows[base + 32 : base + 64]
-                )
-
-        for q in range(0, SEGMENT + 2, 2):
-            if q < SEGMENT:
-                fetch_columns(codes, range(q, q + 2), table, state)
-            if q >= 2:
-                store(q - 2)
-                store(q - 1)
+    state = {}
+
+    def store(codes, segment, q):
+        x = select_columns(codes, q, state)
+        x = x[:COEF] + x[COEF:]
+        rows = jnp.concatenate([x, x], axis=0).T
+        for b in range(2):
+            base = b * 64
+            out_ref[segment * 2 * SEGMENT + 2 * q + b] = jnp.where(
+                left, rows[base : base + 32], rows[base + 32 : base + 64]
+            )
+
+    @pl.loop(0, 8 // FSEGMENTS)
+    def _(trip):
+        segments = [trip * FSEGMENTS + i for i in range(FSEGMENTS)]
+        codes = [slot_codes(cells_ref, counts, segment) for segment in segments]
+        chunks = [(i, q) for i in range(FSEGMENTS) for q in range(0, SEGMENT, 2)]
+        for n in range(len(chunks) + 1):
+            if n > 0:
+                j, r = chunks[n - 1]
+                store(codes[j], segments[j], r)
+            if n < len(chunks):
+                i, q = chunks[n]
+                held = state.pop(("both", chunks[n - 1][1] + 1), None) if n > 0 else None
+                fetch_columns(codes[i], range(q, q + 2), table, state)
+                if held is not None:
+                    state["both", r + 1] = held
+            if n > 0:
+                store(codes[j], segments[j], r + 1)
 
 
 SMEM_SPEC = pl.BlockSpec(memory_space=pltpu.SMEM)
@@ -238,13 +248,14 @@
 
 
 def fetch_index(partners, segment, index, sem):
-    start = pl.multiple_of(jnp.clip(segment, 0, PADDED // SEGMENT - 1) * SEGMENT, SEGMENT)
-    return pltpu.make_async_copy(partners.at[pl.ds(start, SEGMENT)], index, sem)
+    start = (jnp.clip(segment, -1, PADDED // SEGMENT - 1) + 1) * SEGMENT
+    rows = pl.ds(pl.multiple_of(start, SEGMENT), index.shape[0])
+    return pltpu.make_async_copy(partners.at[rows], index, sem)
 
 
 def load_pairs(partners_ref, targets_ref, partners, targets, sem_p, sem_t):
     copies = [
-        pltpu.make_async_copy(partners_ref, partners.at[pl.ds(0, OFFSETS)], sem_p),
+        pltpu.make_async_copy(partners_ref, partners.at[pl.ds(SEGMENT, OFFSETS)], sem_p),
         pltpu.make_async_copy(targets_ref, targets.at[pl.ds(0, OFFSETS)], sem_t),
     ]
     for copy in copies:
@@ -255,8 +266,10 @@
 def finish_pairs(copies, partners, targets):
     for copy in copies:
         copy.wait()
-    for pairs in (partners, targets):
-        pairs[OFFSETS:, :] = jnp.zeros((PADDED - OFFSETS, LANES), jnp.int32)
+    targets[OFFSETS:, :] = jnp.zeros((PADDED - OFFSETS, LANES), jnp.int32)
+    partners[:SEGMENT, :] = jnp.zeros((SEGMENT, LANES), jnp.int32)
+    rest = partners.shape[0] - SEGMENT - OFFSETS
+    partners[SEGMENT + OFFSETS :, :] = jnp.zeros((rest, LANES), jnp.int32)
 
 
 def partner_kernel(
@@ -289,7 +302,7 @@
             bank[pl.ds(pl.multiple_of(i * 128, 128), 128), :] = jnp.zeros((128, LANES), F32)
 
     finish_pairs(pairs, partners, targets)
-    fetch_index(partners, 0, index_e, sem_e).start()
+    fetch_index(partners, -1, index_e, sem_e).start()
     load.wait()
     turn_operators(native, turned)
     keep = pltpu.make_async_copy(turned, turned_ref, sem_ops)
@@ -324,42 +337,47 @@
                 pieces.append(lambda q=q: store(q - 4))
         return pieces
 
-    def scatter(index, update, first):
+    def scatter(index, base, update, first):
         rows = range(first, first + BANKS)
         left = left_half((1, LANES))
         parts = []
         for side, mask in ((0, left), (1, ~left)):
             for bank, row in zip(banks, rows):
-                where = index[row // LANES * 2 + side, row % LANES]
+                where = index[base + row // LANES * 2 + side, row % LANES]
                 view = bank.at[pl.ds(where, 1), :]
                 parts.append((view, mask, view[...], row))
         for view, mask, held, row in parts:
             pltpu.store(view, held + update[row : row + 1, :], mask=mask)
 
-    def both(segment, out, index, update):
+    def both(segment, out, index, base, update):
         codes = pair_codes(targets, counts, segment)
         first = OFFSETS - 1 - segment * SEGMENT
         stage_operators(turned, staged, [jnp.maximum(first - q, 0) for q in range(SEGMENT)])
         pieces = update_pieces(codes, out)
-        batches = [lambda i=i: scatter(index, update, i) for i in range(0, ROWS // 2, BANKS)]
+        batches = [lambda i=i: scatter(index, base, update, i) for i in range(0, ROWS // 2, BANKS)]
         if WEAVE:
             weave(pieces, batches)
         else:
             weave(pieces, [])
             weave([lambda: None], batches)
 
-    @pl.loop(0, STEPS)
+    buffers = (update_a, update_b)
+
+    @pl.loop(0, SEGMENTS // (2 * PARTNER_SPAN))
     def _(step):
-        fetch_index(partners, 2 * step - 1, index_e, sem_e).wait()
-        fetch_index(partners, 2 * step, index_o, sem_o).start()
-        both(2 * step, update_a, index_e, update_b)
-        fetch_index(partners, 2 * step, index_o, sem_o).wait()
-        fetch_index(partners, 2 * step + 1, index_e, sem_e).start()
-        both(2 * step + 1, update_b, index_o, update_a)
-
-    fetch_index(partners, 2 * STEPS - 1, index_e, sem_e).wait()
+        first = 2 * PARTNER_SPAN * step
+        fetch_index(partners, first - 1, index_e, sem_e).wait()
+        fetch_index(partners, first + PARTNER_SPAN - 1, index_o, sem_o).start()
+        for i in range(PARTNER_SPAN):
+            both(first + i, buffers[i % 2], index_e, i * SEGMENT, buffers[1 - i % 2])
+        fetch_index(partners, first + PARTNER_SPAN - 1, index_o, sem_o).wait()
+        fetch_index(partners, first + 2 * PARTNER_SPAN - 1, index_e, sem_e).start()
+        for i in range(PARTNER_SPAN):
+            both(first + PARTNER_SPAN + i, buffers[i % 2], index_o, i * SEGMENT, buffers[1 - i % 2])
+
+    fetch_index(partners, SEGMENTS - 1, index_e, sem_e).wait()
     for first in range(0, OFFSETS % SEGMENT * LANES // 2, BANKS):
-        scatter(index_e, update_b, first)
+        scatter(index_e, 0, update_b, first)
 
     def total(start, size):
         parts = [bank[pl.ds(start, size), :] for bank in banks]
@@ -386,16 +404,16 @@
     keep.wait()
 
 
-def pair_scratch():
+def pair_scratch(span):
     return [
         pltpu.VMEM((PITCH * OFFSETS, LANES), F32),
         pltpu.VMEM((COEF // 2 * SEGMENT, LANES), F32),
-        pltpu.VMEM((PADDED, LANES), jnp.int32),
+        pltpu.VMEM((PADDED + span * SEGMENT, LANES), jnp.int32),
         pltpu.VMEM((PADDED, LANES), jnp.int32),
         pltpu.VMEM((ROWS, LANES), F32),
         pltpu.VMEM((ROWS, LANES), F32),
-        pltpu.SMEM((SEGMENT, LANES), jnp.int32),
-        pltpu.SMEM((SEGMENT, LANES), jnp.int32),
+        pltpu.SMEM((span * SEGMENT, LANES), jnp.int32),
+        pltpu.SMEM((span * SEGMENT, LANES), jnp.int32),
     ] + [pltpu.SemaphoreType.DMA] * 5
 
 
@@ -414,7 +432,7 @@
             pltpu.VMEM((COEF, COEF, OFFSETS), F32),
             pltpu.VMEM((2 * LANES, HALF), BF16),
         ]
-        + pair_scratch()
+        + pair_scratch(PARTNER_SPAN)
         + [pltpu.VMEM((TABLE, LANES), F32)] * BANKS,
         compiler_params=pltpu.CompilerParams(vmem_limit_bytes=VMEM_LIMIT),
         cost_estimate=pl.CostEstimate(
@@ -455,9 +473,9 @@
     fetch_index(partners, 0, index_e, sem_e).start()
     load.wait()
 
-    def gather(index, rows, start, stop):
+    def gather(index, base, rows, start, stop):
         for r in range(start, stop):
-            rows[r : r + 1, :] = table[pl.ds(index[r // LANES, r % LANES], 1), :]
+            rows[r : r + 1, :] = table[pl.ds(index[base + r // LANES, r % LANES], 1), :]
 
     def stage(segment):
         first = segment * SEGMENT
@@ -498,24 +516,29 @@
                     pieces.append(lambda p=(q - 2) // DEPTH, start=start: collect(p, start))
         return pieces
 
-    def both(segment, done, index, rows):
+    def both(segment, done, index, base, rows):
         codes = stage(segment)
         weave(
             sum_pieces(codes, done, SEGMENT),
-            [lambda i=i: gather(index, rows, i, i + BATCH) for i in range(0, ROWS, BATCH)],
+            [lambda i=i: gather(index, base, rows, i, i + BATCH) for i in range(0, ROWS, BATCH)],
         )
 
-    @pl.loop(0, STEPS)
+    buffers = (rows_a, rows_b)
+
+    @pl.loop(0, SEGMENTS // (2 * TARGET_SPAN))
     def _(step):
-        fetch_index(partners, 2 * step, index_e, sem_e).wait()
-        fetch_index(partners, 2 * step + 1, index_o, sem_o).start()
-        both(2 * step - 1, rows_b, index_e, rows_a)
-        fetch_index(partners, 2 * step + 1, index_o, sem_o).wait()
-        fetch_index(partners, 2 * step + 2, index_e, sem_e).start()
-        both(2 * step, rows_a, index_o, rows_b)
-
-    fetch_index(partners, 2 * STEPS, index_e, sem_e).wait()
-    weave(sum_pieces(stage(2 * STEPS - 1), rows_b, OFFSETS % SEGMENT), [])
+        first = 2 * TARGET_SPAN * step
+        fetch_index(partners, first, index_e, sem_e).wait()
+        fetch_index(partners, first + TARGET_SPAN, index_o, sem_o).start()
+        for i in range(TARGET_SPAN):
+            both(first + i - 1, buffers[1 - i % 2], index_e, i * SEGMENT, buffers[i % 2])
+        fetch_index(partners, first + TARGET_SPAN, index_o, sem_o).wait()
+        fetch_index(partners, first + 2 * TARGET_SPAN, index_e, sem_e).start()
+        for i in range(TARGET_SPAN):
+            both(first + TARGET_SPAN + i - 1, buffers[1 - i % 2], index_o, i * SEGMENT, buffers[i % 2])
+
+    fetch_index(partners, SEGMENTS, index_e, sem_e).wait()
+    weave(sum_pieces(stage(SEGMENTS - 1), rows_b, OFFSETS % SEGMENT), [])
     out_ref[...] = total[...]
 
 
@@ -530,7 +553,7 @@
             pltpu.VMEM((TABLE, LANES), F32),
             pltpu.VMEM((HALF, 2 * LANES), F32),
         ]
-        + pair_scratch(),
+        + pair_scratch(TARGET_SPAN),
         compiler_params=pltpu.CompilerParams(vmem_limit_bytes=VMEM_LIMIT),
         cost_estimate=pl.CostEstimate(
             flops=200_000_000_000, bytes_accessed=20_000_000, transcendentals=0

time: 165 us -> 145 us (0.88)
  Pallas kernels: 143 us -> 122 us
    pallas_call x1, Pallas kernels: 71.5 us -> 59.7 us  [partner_sums(): pl.pallas_call(partner_kernel, name='partner_sums', out_shape=(jax.ShapeD...]
    pallas_call x1, Pallas kernels: 58.4 us -> 51.2 us  [target_sums(): pl.pallas_call(target_kernel, name='target_sums', out_shape=jax.ShapeDtyp...]
  transfers between devices with their start and end apart: 2 -> 2, of which waited for: 0 -> 0; matrix products, arithmetic and copies ran while one was open for 0% -> 0% of each run, Pallas kernels for 79% -> 77%
where the time goes in v4:
time: 145 us; the launch traced here: 144 us
  Pallas kernels  122 us (84%)
  starting transfers between devices  22.2 us (15%)
    pallas_call x1, Pallas kernels, partner_sums(): pl.pallas_call(partner_kernel, name='partner_sums', out_shape=(jax.ShapeD...  59.7 us
    pallas_call x1, Pallas kernels, target_sums(): pl.pallas_call(target_kernel, name='target_sums', out_shape=jax.ShapeDtyp...  51.2 us
    all_to_all x2, starting transfers between devices, exchange(): return lax.all_to_all(blocks, axes, split_axis=0, concat_axis=0, tiled=True)  22.2 us
    pallas_call x1, Pallas kernels, finish(): pl.pallas_call(finish_kernel, name='finish', out_shape=jax.ShapeDtypeStru...  5.73 us
    pallas_call x1, Pallas kernels, send_rows(): pl.pallas_call(send_kernel, name='send_rows', out_shape=jax.ShapeDtypeStr...  5.44 us
  transfers between devices with their start and end apart: 2, of which 0 were waited for; matrix products, arithmetic and copies ran while one was open for 0% of the time, Pallas kernels for 77%

profile of v4, /device:TPU:1, one launch (start us, length us, event | category | flops | bytes accessed | tf_op | source)
XLA Modules:
  0.0 144.3 jit_solution(10541345537790652553)
XLA Ops:
  0.0 5.4 %send_rows.1 = f32[128,32,128]{2,1,0:T(8,128)} custom-call(s32[1,128]{1,0:T(1,128)} %counts.7, s32[16,4,128]{2,1,0:T(4,128)} %bitcast.2, f32[64,1024]{1,0:T(8,128)} %multipoles_ref.5), custom_call_target="tpu_custom_call" | custom-call | tf_op jit(solution)/shard_map/send_rows/pallas_call | solution.py:239
  5.4 11.9 %all-to-all-start.1 = ((f32[128,32,128]{2,1,0:T(8,128)}), f32[128,32,128]{2,1,0:T(8,128)}, u32[]{:S(2)}, u32[]{:S(2)}) async-start(f32[128,32,128]{2,1,0:T(8,128)} %send_rows.1), calls=%async_computation.1 | async-start | bytes 4194304 | tf_op jit(solution)/shard_map/all_to_all | solution.py:637
  17.4 59.7 %partner_sums.1 = (f32[1024,128]{1,0:T(8,128)}, f32[128,32,128]{2,1,0:T(8,128)}, f32[10428,128]{1,0:T(8,128)}) custom-call(s32[1,316]{1,0:T(1,128)} %counts.6, s32[316,128]{1,0:T(8,128)} %partners_ref.3, s32[316,128]{1,0:T(8,128)} %targets_ref.3, f32[64,64,316]{2,1,0:T(8,128)} %bitcast.4, f32[64,1024]{1,0:T(8,128)} %multipoles_ref.5), custom_call_target="tpu_custom_call" | custom-call | flops 199999995904 | bytes 20000000 | tf_op jit(solution)/shard_map/partner_sums/pallas_call | solution.py:421
  77.1 0.0 all-to-all-done.1.fetched_ref
  77.1 10.2 %all-to-all-start = ((f32[128,32,128]{2,1,0:T(8,128)}), f32[128,32,128]{2,1,0:T(8,128)}, u32[]{:S(2)}, u32[]{:S(2)}) async-start(f32[128,32,128]{2,1,0:T(8,128)} %get-tuple-element.8), calls=%async_computation | async-start | bytes 4194304 | tf_op jit(solution)/shard_map/all_to_all | solution.py:637
  87.3 51.2 %target_sums.1.target_ref = f32[512,256]{1,0:T(8,128)} custom-call(s32[1,316]{1,0:T(1,128)} %counts.6, s32[316,128]{1,0:T(8,128)} %partners_ref.3, s32[316,128]{1,0:T(8,128)} %targets_ref.3, f32[10428,128]{1,0:T(8,128)} %get-tuple-element.10.turned_ref, f32[64,1024]{1,0:T(8,128)} %multipoles_ref.5, f32[128,32,128]{2,1,0:T(8,128)} %all-to-all-done.1.fetched_ref), custom_call_target="tpu_custom_call" | custom-call | flops 199999995904 | bytes 20000000 | tf_op jit(solution)/shard_map/target_sums/pallas_call | solution.py:546
  138.5 0.0 all-to-all-done.returned_ref
  138.5 5.7 %finish.1 = f32[64,1024]{1,0:T(8,128)} custom-call(s32[1,128]{1,0:T(1,128)} %counts.7, s32[16,4,128]{2,1,0:T(4,128)} %bitcast.3, f32[128,32,128]{2,1,0:T(8,128)} %all-to-all-done.returned_ref, f32[64,1024]{1,0:T(8,128)} %parent_ref.1, f32[1024,128]{1,0:T(8,128)} %get-tuple-element.9.partner_ref, f32[512,256]{1,0:T(8,128)} %target_sums.1.target_ref), custom_call_target="tpu_custom_call" | custom-call | tf_op jit(solution)/shard_map/finish/pallas_call | solution.py:602
Async XLA Ops:
  5.4 71.6 %all-to-all-start.1 = ((f32[128,32,128]{2,1,0:T(8,128)}), f32[128,32,128]{2,1,0:T(8,128)}, u32[]{:S(2)}, u32[]{:S(2)}) async-start(f32[128,32,128]{2,1,0:T(8,128)} %send_rows.1), calls=%async_computation.1 | async-start | bytes 4194304 | tf_op jit(solution)/shard_map/all_to_all | solution.py:637
  77.1 61.5 %all-to-all-start = ((f32[128,32,128]{2,1,0:T(8,128)}), f32[128,32,128]{2,1,0:T(8,128)}, u32[]{:S(2)}, u32[]{:S(2)}) async-start(f32[128,32,128]{2,1,0:T(8,128)} %get-tuple-element.8), calls=%async_computation | async-start | bytes 4194304 | tf_op jit(solution)/shard_map/all_to_all | solution.py:637
